TPU v7x, 256 devices: a whole 4x4x8 slice. The times are simulated.
256 devices in a mesh: contacts: 32 (over y, z), tm: 8 (over x, core).
Axes of the slice: x: 4, y: 4, z: 8, core: 2. Of those that a mesh axis runs over, the one named last changes fastest.
Arguments:
- signal: bfloat16 [8192, 1024], P('contacts', 'tm'), may hold values from -6 to 6
- pos_idx: int32 [8192], P('contacts'), may hold values from 0 to 4095
- live_count: int32 [32], P('contacts'), may hold values from 128 to 256, as said below
- latents: bfloat16 [256, 512], replicated, may hold values from -400 to 400
- pos_table: bfloat16 [4096, 512], replicated, may hold values from -6 to 6
- w_in: bfloat16 [32, 512], replicated, may hold values from -1 to 1
- w_kv: bfloat16 [512, 1024], replicated, may hold values from -0.25 to 0.25
- w_query: bfloat16 [512, 512], replicated, may hold values from -0.25 to 0.25
- w_out: bfloat16 [512, 512], replicated, may hold values from -0.25 to 0.25
- conv_weight: bfloat16 [2, 3, 512, 512], replicated, may hold values from -0.15625 to 0.15625
- conv_bias: float32 [2, 512], replicated, may hold values from -3 to 3
- cotangent: bfloat16 [32, 256, 512], P('tm', 'contacts'), may hold values from -6 to 6
Outputs:
- features: bfloat16 [32, 256, 512], P('tm', 'contacts')
- d_latents: float32 [256, 512], replicated
Inputs may be any that keep to these rules, and one draw needn't show every extreme that they name: The first live_count[b] contacts of block b are valid; some block is full and some block has exactly 128 valid contacts.
All inputs are finite; a program needn't handle non-finite values.
Results may differ from a plain program's by a relative error of at most 0.018.
The roundings to bfloat16 on the way count: a program that leaves them out, or rounds other values in their place, can miss the bound.
Values may be sent and summed in bfloat16 or wider, within the bound.
No kernel may reach another device: no remote copies, remote signals or barrier semaphores. Data moves between devices by JAX's collectives and lax.ppermute only.
A program may use at most 192 MiB of HBM per device.

v0:
```python
import jax
import jax.numpy as jnp
from jax import lax
from jax.sharding import PartitionSpec as P

HD = 64
PATCH = 32
KSIZE = 3
LAYERS = 2


neg_big = -1e30
scale_dot = 0.125


def joined(x, axis, combine):
    everything = jax.tree.map(lambda part: lax.all_gather(part, axis), x)
    first = jax.tree.map(lambda part: part[0], everything)

    def step(k, so_far):
        return combine(so_far, jax.tree.map(lambda part: part[k], everything))

    return lax.fori_loop(1, lax.axis_size(axis), step, first)


def with_halo(x, sides, width):
    for axis, dim in sides:
        peers, length = (lax.axis_size(axis), x.shape[dim])
        up = [(i, (i + 1) % peers) for i in range(peers - 1)]
        down = [(j, i) for i, j in up]
        last = lax.slice_in_dim(x, length - width, length, axis=dim)
        first = lax.slice_in_dim(x, 0, width, axis=dim)
        before = lax.ppermute(last, axis, up)
        after = lax.ppermute(first, axis, down)
        x = jnp.concatenate([before, x, after], axis=dim)
    return x


def silu_slope(pre_act):
    sigmoid_v = jax.nn.sigmoid(pre_act)
    return sigmoid_v * (1.0 + pre_act * (1.0 - sigmoid_v))


def split_heads(values, head_count):
    return values.reshape(values.shape[:-1] + (head_count, values.shape[-1] // head_count))


def combine_parts(part_a, part_b):
    top_a, sum_a, acc_a = part_a
    top_b, sum_b, acc_b = part_b
    top_score = jnp.maximum(top_a, top_b)
    fac_a = jnp.exp(top_a - top_score)
    fac_b = jnp.exp(top_b - top_score)
    head_count = top_score.shape[-1]
    merged = (
        split_heads(acc_a, head_count) * fac_a[..., None]
        + split_heads(acc_b, head_count) * fac_b[..., None]
    )
    return (top_score, sum_a * fac_a + sum_b * fac_b, merged.reshape(acc_a.shape))


def normalize(accum_out, totals):
    head_count = totals.shape[-1]
    return (
        (split_heads(accum_out, head_count) / totals[..., None])
        .reshape(accum_out.shape)
        .astype(jnp.bfloat16)
    )


def conv_apply(source, weight, bias_row, dilation, out_count):
    stacked = jnp.stack(
        [source[j * dilation : j * dilation + out_count] for j in range(KSIZE)], axis=2
    )
    return (
        jnp.einsum("tlji,jio->tlo", stacked, weight, preferred_element_type=jnp.float32) + bias_row
    )


def local(
    signal,
    pos_idx,
    live_count,
    latents,
    pos_table,
    w_in,
    w_kv,
    w_query,
    w_out,
    conv_weight,
    conv_bias,
    cotangent,
):
    con_dev = signal.shape[0]
    pat_dev = signal.shape[1] // PATCH
    model_width = w_query.shape[0]
    head_count = model_width // HD
    lat_rows = latents.shape[0]
    groups = lax.axis_size("contacts")
    lat_dev = lat_rows // groups
    owner_idx = lax.axis_index("contacts")
    is_valid = jnp.arange(con_dev, dtype=jnp.int32) < live_count[0]
    embedded = jnp.einsum(
        "cpt,td->pcd",
        signal.reshape(con_dev, pat_dev, PATCH),
        w_in,
        preferred_element_type=jnp.float32,
    )
    pos_rows = jnp.take(pos_table, pos_idx, axis=0).astype(jnp.float32)
    tokens = (embedded + pos_rows[None]).astype(jnp.bfloat16)
    keyval = jnp.dot(
        tokens.reshape(pat_dev * con_dev, model_width), w_kv, preferred_element_type=jnp.float32
    ).astype(jnp.bfloat16)
    keyval = keyval.reshape(pat_dev // 2, 2, con_dev, 2, head_count, HD)
    queries = (
        jnp.dot(latents, w_query, preferred_element_type=jnp.float32)
        .astype(jnp.bfloat16)
        .reshape(lat_rows, head_count, HD)
    )

    def masked_scores(key_block):
        scores = (
            jnp.einsum("ihe,pche->phic", queries, key_block, preferred_element_type=jnp.float32)
            * scale_dot
        )
        return jnp.where(is_valid, scores, neg_big)

    def attend(kv_block):
        scores = masked_scores(kv_block[:, :, 0])
        top_score = jnp.max(scores, axis=3)
        weights = jnp.where(is_valid, jnp.exp(scores - top_score[..., None]), 0.0)
        totals = jnp.sum(weights, axis=3)
        accum_out = jnp.einsum(
            "phic,pche->pihe",
            weights.astype(jnp.bfloat16),
            kv_block[:, :, 1],
            preferred_element_type=jnp.float32,
        )
        return (
            jnp.swapaxes(top_score, 1, 2),
            jnp.swapaxes(totals, 1, 2),
            accum_out.reshape(2, lat_rows, model_width),
        )

    top_score, totals, accum_out = lax.map(attend, keyval)
    top_score = top_score.reshape(pat_dev, lat_rows, head_count)
    totals = totals.reshape(pat_dev, lat_rows, head_count)
    accum_out = accum_out.reshape(pat_dev, lat_rows, model_width)
    top_all, total_all, acc_all = joined((top_score, totals, accum_out), "contacts", combine_parts)
    attended_all = normalize(acc_all, total_all)
    attended = lax.dynamic_slice_in_dim(attended_all, owner_idx * lat_dev, lat_dev, 1)
    start_x = (
        jnp.dot(
            attended.reshape(pat_dev * lat_dev, model_width),
            w_out,
            preferred_element_type=jnp.float32,
        )
        .astype(jnp.bfloat16)
        .reshape(pat_dev, lat_dev, model_width)
    )
    hidden_list = []
    current = start_x
    for layer_no in range(LAYERS):
        dilation = 2**layer_no
        padded = with_halo(current, (("tm", 0),), dilation * (KSIZE // 2))
        pre_act = conv_apply(padded, conv_weight[layer_no], conv_bias[layer_no], dilation, pat_dev)
        current = (current.astype(jnp.float32) + jax.nn.silu(pre_act)).astype(jnp.bfloat16)
        hidden_list.append(pre_act)
    grad_now = cotangent.astype(jnp.float32)
    for layer_no in reversed(range(LAYERS)):
        dilation = 2**layer_no
        grad_pre = (grad_now * silu_slope(hidden_list[layer_no])).astype(jnp.bfloat16)
        padded = with_halo(grad_pre, (("tm", 0),), dilation * (KSIZE // 2))
        stacked = jnp.stack(
            [
                padded[(KSIZE - 1 - j) * dilation : (KSIZE - 1 - j) * dilation + pat_dev]
                for j in range(KSIZE)
            ],
            axis=2,
        )
        grad_now = grad_now + jnp.einsum(
            "tljo,jio->tli", stacked, conv_weight[layer_no], preferred_element_type=jnp.float32
        )
    grad_att = lax.dot_general(
        grad_now.astype(jnp.bfloat16).reshape(pat_dev * lat_dev, model_width),
        w_out,
        (((1,), (1,)), ((), ())),
        preferred_element_type=jnp.float32,
    )
    grad_att = grad_att.astype(jnp.bfloat16).reshape(pat_dev, lat_dev, model_width)
    grad_all = lax.all_gather(grad_att, "contacts", axis=1, tiled=True)
    delta_row = jnp.sum(
        split_heads(grad_all.astype(jnp.float32), head_count)
        * split_heads(attended_all.astype(jnp.float32), head_count),
        axis=3,
    )

    def back_block(dq_sum, parts):
        kv_block, grad_block, top_block, total_block, delta_block = parts
        key_block = kv_block[:, :, 0]
        scores = masked_scores(key_block)
        top_now = jnp.swapaxes(top_block, 1, 2)
        total_now = jnp.swapaxes(total_block, 1, 2)
        prob_vals = jnp.where(
            is_valid, jnp.exp(scores - top_now[..., None]) / total_now[..., None], 0.0
        )
        grad_prob = jnp.einsum(
            "pihe,pche->phic",
            split_heads(grad_block, head_count),
            kv_block[:, :, 1],
            preferred_element_type=jnp.float32,
        )
        delta_now = jnp.swapaxes(delta_block, 1, 2)
        dscore = (prob_vals * (grad_prob - delta_now[..., None])).astype(jnp.bfloat16)
        return (
            dq_sum
            + jnp.einsum("phic,pche->ihe", dscore, key_block, preferred_element_type=jnp.float32),
            None,
        )

    pairs = pat_dev // 2
    dq_sum, unused = lax.scan(
        back_block,
        jnp.zeros((lat_rows, head_count, HD), jnp.float32),
        (
            keyval,
            grad_all.reshape(pairs, 2, lat_rows, model_width),
            top_all.reshape(pairs, 2, lat_rows, head_count),
            total_all.reshape(pairs, 2, lat_rows, head_count),
            delta_row.reshape(pairs, 2, lat_rows, head_count),
        ),
    )
    query_grad = lax.psum((dq_sum * scale_dot).reshape(lat_rows, model_width), ("contacts", "tm"))
    d_latents = lax.dot_general(
        query_grad.astype(jnp.bfloat16),
        w_query,
        (((1,), (1,)), ((), ())),
        preferred_element_type=jnp.float32,
    )
    return (current, d_latents)


def solution(mesh):
    in_specs = (
        P("contacts", "tm"),
        P("contacts"),
        P("contacts"),
        P(),
        P(),
        P(),
        P(),
        P(),
        P(),
        P(),
        P(),
        P("tm", "contacts", None),
    )
    out_specs = (P("tm", "contacts", None), P())
    return jax.shard_map(local, mesh=mesh, in_specs=in_specs, out_specs=out_specs, check_vma=False)
```

profile of v0, /device:TPU:1, one launch (start us, length us, event | category | flops | bytes accessed | tf_op | source)
XLA Modules:
  0.0 1136.9 jit_solution(8328710909862078384)
XLA Ops:
  9.6 3.9 gather_fusion
  15.5 4.0 reshape.142
  19.5 5.5 copy.76
  25.4 12.2 %while.46 = (s32[]{:T(128)}, f32[2,2,256,8]{2,3,1,0:T(8,128)S(1)}, f32[2,2,256,8]{2,3,1,0:T(8,128)S(1)}, f32[2,2,256,512]{3,2,1,0:T(8,128)}, bf16[2,2,256,2,8,64...) while((s32[]{:T(128)}, f32[2,2,256,8]{2,3,1,0:T(8,128)S(1)}, ...), condition=%wide.region_3.4_spmd.clone, body=%wide.region_0.3_spmd.clone.sunk | while | flops 277864704 | bytes 21349984 | solution.py:145
  39.8 73.7 %all-gather.7.cloned.1.call-done = f32[32,4,256,8]{2,3,1,0:T(8,128)} async-done(((f32[1,4,256,8]{2,3,1,0:T(8,128)}), f32[32,4,256,8]{2,3,1,0:T(8,128)}) %all-gather.7.cloned.1.call-update) | async-done | bytes 1048592 | tf_op jit(solution)/shard_map/all_gather | solution.py:17
  114.2 76.3 %all-gather.5.cloned.1.call-done = f32[32,4,256,8]{2,3,1,0:T(8,128)} async-done(((f32[1,4,256,8]{2,3,1,0:T(8,128)}), f32[32,4,256,8]{2,3,1,0:T(8,128)}) %all-gather.5.cloned.1.call-update) | async-done | bytes 1048592 | tf_op jit(solution)/shard_map/all_gather | solution.py:17
  191.3 434.8 %all-gather.9.cloned.1.call-done = f32[32,4,256,512]{3,2,1,0:T(8,128)} async-done(((f32[1,4,256,512]{3,2,1,0:T(8,128)}), f32[32,4,256,512]{3,2,1,0:T(8,128)}) %all-gather.9.cloned.1.call-update) | async-done | bytes 67108880 | tf_op jit(solution)/shard_map/all_gather | solution.py:17
  629.7 282.2 %while.45 = (s32[]{:T(128)}, f32[4,256,8]{1,2,0:T(8,128)S(1)}, f32[4,256,8]{1,2,0:T(8,128)S(1)}, f32[4,256,512]{1,2,0:T(8,128)}, f32[32,4,256,8]{2,3,1,0:T(8,128...) while((s32[]{:T(128)}, f32[4,256,8]{1,2,0:T(8,128)S(1)}, ...), condition=%wide.region_5.6_spmd, body=%wide.region_4.5_spmd.sunk | while | flops 1622021 | bytes 15007895 | solution.py:23
  635.5 3.2 fusion.147
  639.6 3.1 constant_dynamic-slice_fusion.10
  644.6 3.2 fusion.147
  648.7 3.1 constant_dynamic-slice_fusion.10
  653.7 3.2 fusion.147
  657.8 3.1 constant_dynamic-slice_fusion.10
  662.8 3.2 fusion.147
  666.9 3.1 constant_dynamic-slice_fusion.10
  671.9 3.2 fusion.147
  676.0 3.1 constant_dynamic-slice_fusion.10
  681.1 3.2 fusion.147
  690.2 3.2 fusion.147
  699.3 3.2 fusion.147
  703.3 3.1 constant_dynamic-slice_fusion.10
  708.4 3.2 fusion.147
  712.4 3.1 constant_dynamic-slice_fusion.10
  717.5 3.2 fusion.147
  721.5 3.1 constant_dynamic-slice_fusion.10
  726.6 3.2 fusion.147
  730.6 3.1 constant_dynamic-slice_fusion.10
  735.7 3.2 fusion.147
  744.8 3.2 fusion.147
  753.9 3.2 fusion.147
  757.9 3.1 constant_dynamic-slice_fusion.10
  763.0 3.2 fusion.147
  767.0 3.1 constant_dynamic-slice_fusion.10
  772.1 3.2 fusion.147
  776.1 3.1 constant_dynamic-slice_fusion.10
  781.2 3.2 fusion.147
  785.3 3.1 constant_dynamic-slice_fusion.10
  790.3 3.2 fusion.147
  799.4 3.2 fusion.147
  808.5 3.2 fusion.147
  812.6 3.1 constant_dynamic-slice_fusion.10
  817.6 3.2 fusion.147
  821.7 3.1 constant_dynamic-slice_fusion.10
  826.7 3.2 fusion.147
  830.8 3.1 constant_dynamic-slice_fusion.10
  835.8 3.2 fusion.147
  839.9 3.1 constant_dynamic-slice_fusion.10
  844.9 3.2 fusion.147
  854.0 3.2 fusion.147
  863.1 3.2 fusion.147
  872.2 3.2 fusion.147
  881.4 3.2 fusion.147
  890.5 3.2 fusion.147
  899.6 3.2 fusion.147
  908.7 3.2 fusion.147
  914.3 4.5 collective-permute-start
  935.6 3.6 collective-permute-start.5
  942.6 4.4 collective-permute-start.7
  950.5 69.0 %all-gather.11.cloned.1.call-done = bf16[4,256,512]{2,0,1:T(4,128)(2,1)} async-done(((bf16[4,8,512]{2,0,1:T(4,128)(2,1)}), bf16[4,256,512]{2,0,1:T(4,128)(2,1)}) %all-gather.11.cloned.1.call-update) | async-done | bytes 1048592 | tf_op jit(solution)/shard_map/all_gather | solution.py:191
  1022.1 23.4 %while.47 = (s32[]{:T(128)}, f32[256,8,64]{0,2,1:T(8,128)}, bf16[2,2,256,2,8,64]{2,5,1,4,3,0:T(8,128)(2,1)}, bf16[256,8,64]{0,2,1:T(8,128)(2,1)S(1)}, f32[2,2,25...) while((s32[]{:T(128)}, f32[256,8,64]{0,2,1:T(8,128)}, ...), condition=%wide.region_8.9_spmd.clone, body=%wide.region_7.8_spmd.clone.sunk | while | flops 411304192 | bytes 15189387 | solution.py:222
  1028.5 5.3 fusion.155
  1040.1 5.5 fusion.155
  1046.7 82.5 %all-reduce.1 = bf16[256,512]{0,1:T(8,128)(2,1)S(1)} all-reduce(f32[256,512]{0,1:T(8,128)S(1)} %bitcast.319), channel_id=1, replica_groups=mesh['contacts'=32,'tm'=8] {'contacts','tm'}, use_global_device_ids=true, to_apply=%region_9.10 | all-reduce | flops 131072 | bytes 786432 | tf_op jit(solution)/shard_map/psum | solution.py:233
  (192 shorter events, 195.7 us)
Async XLA Ops:
  7.2 7.0 copy-start
  7.2 6.5 copy-start.6
  7.2 106.3 %all-gather.7.cloned.1.call-start = ((), (), s32[]{:S(2)}) async-start(), calls=%async_computation.1 | async-start | bytes 1081344 | tf_op jit(solution)/shard_map/all_gather | solution.py:17
  19.4 5.5 copy-start.1
  19.4 5.5 copy-start.5
  37.6 0.6 copy-start.8
  37.6 0.7 copy-start.7
  38.2 152.3 %all-gather.5.cloned.1.call-start = ((), (), s32[]{:S(2)}) async-start(), calls=%async_computation | async-start | bytes 1081344 | tf_op jit(solution)/shard_map/all_gather | solution.py:17
  39.0 587.1 %all-gather.9.cloned.1.call-start = ((), (), s32[]{:S(2)}) async-start(), calls=%async_computation.2 | async-start | bytes 69206016 | tf_op jit(solution)/shard_map/all_gather | solution.py:17
  39.7 979.8 %all-gather.11.cloned.1.call-start = ((), (), s32[]{:S(2)}) async-start(), calls=%async_computation.3 | async-start | bytes 1081344 | tf_op jit(solution)/shard_map/all_gather | solution.py:191
  911.9 2.2 copy-start.3
  911.9 8.9 copy-start.9
  914.1 18.5 %copy-start.4 = (bf16[2,3,512,512]{3,2,1,0:T(8,128)(2,1)S(1)}, bf16[2,3,512,512]{3,2,1,0:T(8,128)(2,1)}, u32[]{:S(2)}) copy-start(bf16[2,3,512,512]{3,2,1,0:T(8,128)(2,1)} %param.27) | copy-start | bytes 9437188
  914.1 18.6 %copy-start.10 = (bf16[4,8,512]{2,1,0:T(8,128)(2,1)S(1)}, bf16[4,8,512]{2,1,0:T(8,128)(2,1)}, u32[]{:S(2)}) copy-start(bf16[4,8,512]{2,1,0:T(8,128)(2,1)} %param.29) | copy-start | bytes 98308
  914.3 6.5 collective-permute-start
  918.9 5.0 collective-permute-start.1
  925.7 4.3 collective-permute-start.2
  927.6 5.1 collective-permute-start.3
  933.7 5.6 collective-permute-start.4
  935.6 4.5 collective-permute-start.5
  940.7 6.3 collective-permute-start.6
  942.6 5.0 collective-permute-start.7
  1045.6 83.6 %copy-start.2 = (bf16[512,512]{1,0:T(8,128)(2,1)S(1)}, bf16[512,512]{1,0:T(8,128)(2,1)}, u32[]{:S(2)}) copy-start(bf16[512,512]{1,0:T(8,128)(2,1)} %param.25) | copy-start | bytes 1572868
Sparse Core Ops, SparseCore 0:
  38.4 75.0 all-gather.6
  116.6 73.8 all-gather.4
  193.1 432.8 all-gather.8
  950.6 68.8 all-gather.10
where the time goes:
time: 1140 us
  waiting for transfers between devices  662 us (58%)
  local copies, waits for them, and re-layouts  191 us (17%)
  other arithmetic  136 us (12%)
  blocking collectives  82.5 us (7%)
  matrix products  28.2 us (2%)
  starting transfers between devices  22.8 us (2%)
  between operations  14.1 us (1%)
    all_gather x3, waiting for transfers between devices, joined(): everything = jax.tree.map(lambda part: lax.all_gather(part, axis), x)  585 us
    dynamic_slice x62, local copies, waits for them, and re-layouts, step(): return combine(so_far, jax.tree.map(lambda part: part[k], everything))  156 us
    add x31, other arithmetic, combine_parts(): split_heads(acc_a, head_count) * fac_a[..., None]  100 us
    psum x1, blocking collectives, local(): lax.psum((dq_sum * scale_dot).reshape(lat_rows, model_width), ('contacts'...  82.5 us
    all_gather x1, waiting for transfers between devices, local(): grad_all = lax.all_gather(grad_att, 'contacts', axis=1, tiled=True)  69 us
    add x31, other arithmetic, combine_parts(): sum_a * fac_a + sum_b * fac_b  25.1 us
  transfers between devices with their start and end apart: 12, of which 8 were waited for; matrix products, arithmetic and copies ran while one was open for 0% of the time, Pallas kernels for 0%

commit v1 on v0

v1 whole, which is shorter than its diff:
```python
import jax
import jax.numpy as jnp
from jax import lax
from jax.experimental import pallas as pl
from jax.experimental.pallas import tpu as pltpu
from jax.sharding import Mesh
from jax.sharding import PartitionSpec as P

HD = 64
PATCH = 32
KSIZE = 3
LAYERS = 2

neg_big = -1e30
scale_dot = 0.125

bf16 = jnp.bfloat16
f32 = jnp.float32

NY, NZH, NZL, NTM = 4, 4, 2, 8


def nt_dot(a, b):
    return lax.dot_general(a, b, (((1,), (1,)), ((), ())), preferred_element_type=f32)


def nn_dot(a, b):
    return jnp.dot(a, b, preferred_element_type=f32)


def head_of_lane(shape):
    return lax.broadcasted_iota(jnp.int32, shape, len(shape) - 1) // HD


def spread_heads(rows, heads):
    head = head_of_lane(rows.shape)
    zero = jnp.zeros_like(rows)
    return jnp.concatenate([jnp.where(head == h, rows, zero) for h in range(heads)], axis=0)


def collect_heads(blocks, heads):
    r = blocks.shape[0] // heads
    head = head_of_lane((r, blocks.shape[1]))
    out = blocks[:r]
    for h in range(1, heads):
        out = jnp.where(head == h, blocks[h * r : (h + 1) * r], out)
    return out


def columns_to_lanes(column, heads, first, base):
    r = base.shape[0]
    lane = lax.broadcasted_iota(jnp.int32, base.shape, 1)
    for h in range(heads):
        base = jnp.where(lane == first + h, column[h * r : (h + 1) * r], base)
    return base


def lanes_to_column(stats, heads, first):
    return jnp.concatenate([stats[:, first + h : first + h + 1] for h in range(heads)], axis=0)


def lanes_to_columns_wide(stats, heads, first):
    r = stats.shape[0]
    head = head_of_lane((r, heads * HD))
    out = jnp.broadcast_to(stats[:, first : first + 1], (r, heads * HD))
    for h in range(1, heads):
        out = jnp.where(head == h, stats[:, first + h : first + h + 1], out)
    return out


def silu_slope(pre_act):
    sigmoid_v = jax.nn.sigmoid(pre_act)
    return sigmoid_v * (1.0 + pre_act * (1.0 - sigmoid_v))


def rounded(value):
    return value.astype(bf16).astype(f32)


def pos_kernel(idx_ref, table_ref, out_ref):
    idx = idx_ref[...]
    n, pos = idx.shape[0], table_ref.shape[0]
    step = 512
    acc = jnp.zeros(out_ref.shape, f32)
    for k in range(pos // step):
        ids = lax.broadcasted_iota(jnp.int32, (n, step), 1) + k * step
        hot = jnp.where(ids == idx, 1.0, 0.0).astype(bf16)
        acc = acc + nn_dot(hot, table_ref[k * step : (k + 1) * step, :])
    out_ref[...] = acc.astype(bf16)


def pos_rows(idx, table):
    rows, width = idx.shape[0], table.shape[1]
    tile = 256
    return pl.pallas_call(
        pos_kernel,
        grid=(rows // tile,),
        in_specs=[
            pl.BlockSpec((tile, 1), lambda i: (i, 0)),
            pl.BlockSpec(table.shape, lambda i: (0, 0), pipeline_mode=pl.Buffered(1)),
        ],
        out_specs=pl.BlockSpec((tile, width), lambda i: (i, 0)),
        out_shape=jax.ShapeDtypeStruct((rows, width), bf16),
        name="pos_rows",
    )(idx, table)


def forward_kernel(sig_ref, pos_ref, valid_ref, q_ref, w_in_ref, w_kv_ref, kv_ref, part_ref, score_ref):
    heads = q_ref.shape[1] // HD
    width = q_ref.shape[1]
    contacts = sig_ref.shape[0]
    step = 256
    window = pl.program_id(0)
    w_in = w_in_ref[...]
    tall = jnp.concatenate([w_in] * (sig_ref.shape[1] // PATCH), axis=0)
    own = lax.broadcasted_iota(jnp.int32, tall.shape, 0) // PATCH == window
    w_here = jnp.where(own, tall, jnp.zeros_like(tall))
    q_wide = spread_heads(q_ref[...], heads)
    for k in range(contacts // step):
        rows = slice(k * step, (k + 1) * step)
        embedded = nn_dot(sig_ref[rows, :], w_here)
        tokens = (embedded + pos_ref[rows, :].astype(f32)).astype(bf16)
        keyval = nn_dot(tokens, w_kv_ref[...]).astype(bf16)
        kv_ref[0, rows, :] = keyval
        scores = nt_dot(q_wide, keyval[:, :width]) * scale_dot
        score_ref[:, rows] = jnp.where(valid_ref[:, rows] > 0.0, scores, neg_big)
    top = jnp.max(score_ref[...], axis=1, keepdims=True)
    totals = jnp.zeros_like(top)
    accum = jnp.zeros((q_wide.shape[0], width), f32)
    for k in range(contacts // step):
        rows = slice(k * step, (k + 1) * step)
        weights = jnp.exp(score_ref[:, rows] - top)
        totals = totals + jnp.sum(weights, axis=1, keepdims=True)
        accum = accum + nn_dot(weights.astype(bf16), kv_ref[0, rows, width:])
    mixed = collect_heads(accum, heads)
    lat = mixed.shape[0]
    stats = jnp.zeros((lat, 128), f32)
    stats = columns_to_lanes(top, heads, 0, stats)
    stats = columns_to_lanes(totals, heads, heads, stats)
    each = part_ref.shape[2]
    for s in range(part_ref.shape[0]):
        part_ref[s, 0, :, :width] = mixed[s * each : (s + 1) * each]
        part_ref[s, 0, :, width:] = stats[s * each : (s + 1) * each]


def forward_attention(sig, pos, valid, q, w_in, w_kv, slots):
    contacts, width = pos.shape
    windows = sig.shape[1] // PATCH
    lat = q.shape[0]
    whole = lambda a: pl.BlockSpec(a.shape, lambda p: (0,) * a.ndim, pipeline_mode=pl.Buffered(1))
    return pl.pallas_call(
        forward_kernel,
        grid=(windows,),
        in_specs=[whole(sig), whole(pos), whole(valid), whole(q), whole(w_in), whole(w_kv)],
        out_specs=[
            pl.BlockSpec((1, contacts, 2 * width), lambda p: (p, 0, 0)),
            pl.BlockSpec((slots, 1, lat // slots, width + 128), lambda p: (0, p, 0, 0)),
        ],
        out_shape=[
            jax.ShapeDtypeStruct((windows, contacts, 2 * width), bf16),
            jax.ShapeDtypeStruct((slots, windows, lat // slots, width + 128), f32),
        ],
        scratch_shapes=[pltpu.VMEM((lat * (width // HD), contacts), f32)],
        name="forward_attention",
    )(sig, pos, valid, q, w_in, w_kv)


def combine_kernel(*refs):
    *part_refs, att_ref, stats_ref = refs
    rows, width = att_ref.shape
    heads = width // HD
    lane = lax.broadcasted_iota(jnp.int32, (rows, 128), 1)
    parts = [ref[...].reshape(rows, width + 128) for ref in part_refs]
    top = parts[0][:, width:]
    for part in parts[1:]:
        top = jnp.maximum(top, part[:, width:])
    totals = jnp.zeros((rows, 128), f32)
    accum = jnp.zeros((rows, width), f32)
    for part in parts:
        factor = jnp.exp(jnp.where(lane < heads, part[:, width:] - top, 0.0))
        totals = totals + factor * pltpu.roll(part[:, width:], 128 - heads, 1)
        accum = accum + part[:, :width] * lanes_to_columns_wide(factor, heads, 0)
    totals = jnp.where(lane < heads, totals, 1.0)
    att_ref[...] = (accum / lanes_to_columns_wide(totals, heads, 0)).astype(bf16)
    stats_ref[...] = jnp.where(lane < heads, top, pltpu.roll(1.0 / totals, heads, 1))


def combine(parts):
    windows, each, wide = parts[0].shape
    rows = windows * each
    return pl.pallas_call(
        combine_kernel,
        out_shape=[
            jax.ShapeDtypeStruct((rows, wide - 128), bf16),
            jax.ShapeDtypeStruct((rows, 128), f32),
        ],
        name="combine_parts",
    )(*parts)


def conv_kernel(
    tm_ref, l2_ref, l4_ref, own_ref, r4_ref, r2_ref, stats_ref, cl_ref, cot_ref, cr_ref,
    w_out_ref, conv_ref, bias_ref, feat_ref, msg_ref,
):
    rows, width = own_ref.shape
    heads = width // HD
    windows = 4
    each = rows // windows
    reach = 6
    first = tm_ref[0] * windows - reach
    total_windows = NTM * windows

    def inside(lo, count):
        w = lax.broadcasted_iota(jnp.int32, (count * each, width), 0) // each + (first + lo)
        return jnp.logical_and(w >= 0, w < total_windows)

    att = jnp.concatenate([r[...].astype(f32) for r in (l2_ref, l4_ref, own_ref, r4_ref, r2_ref)], axis=0)
    w_out = w_out_ref[...]
    x0 = rounded(nn_dot(att.astype(bf16), w_out))
    n0 = 14 * each
    pre0 = bias_ref[0:1, :] + sum(nn_dot(x0[j * each : j * each + n0].astype(bf16), conv_ref[0, j]) for j in range(KSIZE))
    x1 = rounded(x0[each : each + n0] + jax.nn.silu(pre0))
    x1 = jnp.where(inside(1, 14), x1, 0.0)
    n1 = 10 * each
    pre1 = bias_ref[1:2, :] + sum(nn_dot(x1[2 * j * each : 2 * j * each + n1].astype(bf16), conv_ref[1, j]) for j in range(KSIZE))
    feat_ref[...] = (x1[5 * each : 9 * each] + jax.nn.silu(pre1[3 * each : 7 * each])).astype(bf16)
    g2 = jnp.concatenate([r[...].astype(f32) for r in (cl_ref, cot_ref, cr_ref)], axis=0)
    gpre1 = rounded(g2 * silu_slope(pre1))
    n2 = 6 * each
    g1 = g2[2 * each : 8 * each] + sum(
        nt_dot(gpre1[(4 - 2 * j) * each : (4 - 2 * j) * each + n2].astype(bf16), conv_ref[1, j]) for j in range(KSIZE)
    )
    gpre0 = rounded(g1 * silu_slope(pre0[4 * each : 10 * each]))
    gpre0 = jnp.where(inside(5, 6), gpre0, 0.0)
    g0 = g1[each : 5 * each] + sum(
        nt_dot(gpre0[(2 - j) * each : (2 - j) * each + rows].astype(bf16), conv_ref[0, j]) for j in range(KSIZE)
    )
    grad_att = rounded(nt_dot(g0.astype(bf16), w_out))
    msg_ref[:, :width] = grad_att.astype(bf16)
    product = grad_att * own_ref[...].astype(f32)
    head = head_of_lane((rows, width))
    lane = lax.broadcasted_iota(jnp.int32, (rows, 128), 1)
    stats = stats_ref[...]
    for h in range(heads):
        delta = jnp.sum(jnp.where(head == h, product, 0.0), axis=1, keepdims=True)
        stats = jnp.where(lane == 2 * heads + h, delta, stats)
    stats = jnp.where(lane < 3 * heads, stats, 0.0)
    high = rounded(stats)
    middle = rounded(stats - high)
    low = (stats - high) - middle
    msg_ref[:, width:] = (high + pltpu.roll(middle, 32, 1) + pltpu.roll(low, 64, 1)).astype(bf16)


def conv_stack(tm, halo, own, stats, cots, w_out, conv_weight, conv_bias):
    rows, width = own.shape
    l2, l4, r4, r2 = halo
    cl, cot, cr = cots
    vmem = pl.BlockSpec(memory_space=pltpu.VMEM)
    return pl.pallas_call(
        conv_kernel,
        in_specs=[pl.BlockSpec(memory_space=pltpu.SMEM)] + [vmem] * 12,
        out_specs=[vmem, vmem],
        out_shape=[
            jax.ShapeDtypeStruct((rows, width), bf16),
            jax.ShapeDtypeStruct((rows, width + 128), bf16),
        ],
        name="conv_stack",
    )(tm, l2, l4, own, r4, r2, stats, cl, cot, cr, w_out, conv_weight, conv_bias)


def backward_kernel(zh_ref, kv_ref, valid_ref, q_ref, *refs):
    *msg_refs, dq_ref, acc_ref = refs
    width = q_ref.shape[1]
    heads = width // HD
    contacts = kv_ref.shape[1]
    step = 256
    window = pl.program_id(0)
    msg = jnp.concatenate([r[0].astype(f32) for r in msg_refs], axis=0)
    terms = msg[:, width:]
    stats = terms + pltpu.roll(terms, 96, 1) + pltpu.roll(terms, 64, 1)
    top = lanes_to_column(stats, heads, 0)
    inverse = lanes_to_column(stats, heads, heads)
    delta = lanes_to_column(stats, heads, 2 * heads)
    grad_wide = spread_heads(msg[:, :width].astype(bf16), heads)
    q_wide = spread_heads(q_ref[...], heads)
    accum = jnp.zeros((q_wide.shape[0], width), f32)
    for k in range(contacts // step):
        rows = slice(k * step, (k + 1) * step)
        key_rows = kv_ref[0, rows, :width]
        scores = nt_dot(q_wide, key_rows) * scale_dot
        scores = jnp.where(valid_ref[:, rows] > 0.0, scores, neg_big)
        prob = jnp.exp(scores - top) * inverse
        grad_prob = nt_dot(grad_wide, kv_ref[0, rows, width:])
        dscore = (prob * (grad_prob - delta)).astype(bf16)
        accum = accum + nn_dot(dscore, key_rows)

    @pl.when(window == 0)
    def _():
        acc_ref[...] = accum

    @pl.when(window > 0)
    def _():
        acc_ref[...] = acc_ref[...] + accum

    @pl.when(window == pl.num_programs(0) - 1)
    def _():
        dq = collect_heads(acc_ref[...], heads) * scale_dot
        slots = len(msg_refs)
        each = dq.shape[0] // slots
        for s in range(slots):
            place = pl.multiple_of(((zh_ref[0] + (slots - s)) % slots) * each, each)
            dq_ref[pl.ds(place, each), :] = dq[s * each : (s + 1) * each]


def backward_attention(zh, kv, valid, q, msgs):
    windows, contacts, wide = kv.shape
    lat, width = q.shape
    heads = width // HD
    whole = lambda a: pl.BlockSpec(a.shape, lambda p: (0,) * a.ndim, pipeline_mode=pl.Buffered(1))
    return pl.pallas_call(
        backward_kernel,
        grid=(windows,),
        in_specs=[
            pl.BlockSpec(memory_space=pltpu.SMEM),
            pl.BlockSpec((1, contacts, wide), lambda p: (p, 0, 0)),
            whole(valid),
            whole(q),
        ]
        + [pl.BlockSpec((1,) + m.shape[1:], lambda p: (p, 0, 0)) for m in msgs],
        out_specs=pl.BlockSpec((lat, width), lambda p: (0, 0)),
        out_shape=jax.ShapeDtypeStruct((lat, width), f32),
        scratch_shapes=[pltpu.VMEM((lat * heads, width), f32)],
        name="backward_attention",
    )(zh, kv, valid, q, *msgs)


def shift(axis, count, by):
    return [(i, (i + by) % count) for i in range(count)]


def local(
    signal, pos_idx, live_count, latents, pos_table, w_in, w_kv, w_query, w_out,
    conv_weight, conv_bias, cotangent,
):
    con_dev = signal.shape[0]
    pat_dev = signal.shape[1] // PATCH
    width = w_query.shape[0]
    lat_rows = latents.shape[0]
    y, zh, zl, tm = (lax.axis_index(a) for a in ("y", "zh", "zl", "tm"))
    lat_dev = lat_rows // (NY * NZH * NZL)

    up1 = [(i, i + 1) for i in range(NTM - 1)]
    down1 = [(i + 1, i) for i in range(NTM - 1)]
    up2 = [(i, i + 2) for i in range(NTM - 2)]
    down2 = [(i + 2, i) for i in range(NTM - 2)]
    cot = cotangent.reshape(pat_dev * lat_dev, width)

    high = (pos_idx // 64).astype(bf16).reshape(-1, signal.shape[1])
    low = (pos_idx % 64).astype(bf16).reshape(-1, signal.shape[1])
    live = jnp.broadcast_to(live_count.astype(bf16)[:, None], (4, signal.shape[1]))
    message = jnp.concatenate([signal, high, low, live], axis=0)
    other = lax.ppermute(message, "zl", shift("zl", NZL, 1))
    pair = jnp.stack([message, other])
    group = jnp.concatenate([pair] + [lax.ppermute(pair, "y", shift("y", NY, s)) for s in range(1, NY)], axis=0)
    blocks = group.shape[0]
    sig = group[:, :con_dev].reshape(blocks * con_dev, -1)
    tail = group[:, con_dev:].astype(f32)
    half = high.shape[0]
    idx = (tail[:, :half] * 64.0 + tail[:, half : 2 * half]).astype(jnp.int32).reshape(blocks * con_dev, 1)
    lives = tail[:, 2 * half, :1]
    valid = (jnp.arange(con_dev, dtype=jnp.int32)[None, :].astype(f32) < lives).astype(f32)
    valid = valid.reshape(1, blocks * con_dev)

    cot_left = lax.ppermute(cot[lat_dev:], "tm", up1)
    cot_right = lax.ppermute(cot[: 3 * lat_dev], "tm", down1)

    by_owner = latents.reshape(NY, NZH, NZL, lat_dev, width)
    mine = lax.dynamic_slice(by_owner, (y, 0, zl, 0, 0), (1, NZH, 1, lat_dev, width)).reshape(NZH, lat_dev, width)
    slots = jnp.stack([lax.dynamic_index_in_dim(mine, (zh + NZH - s) % NZH, 0, False) for s in range(NZH)])
    queries = nn_dot(slots.reshape(NZH * lat_dev, width), w_query).astype(bf16)

    pos = pos_rows(idx, pos_table)
    kv, parts = forward_attention(sig, pos, valid, queries, w_in, w_kv, NZH)
    received = [lax.ppermute(parts[s], "zh", shift("zh", NZH, -s)) for s in range(1, NZH)]
    att, stats = combine([parts[0]] + received)

    left4 = lax.ppermute(att, "tm", up1)
    right4 = lax.ppermute(att, "tm", down1)
    left2 = lax.ppermute(att[2 * lat_dev :], "tm", up2)
    right2 = lax.ppermute(att[: 2 * lat_dev], "tm", down2)
    features, msg = conv_stack(
        tm.reshape(1), (left2, left4, right4, right2), att, stats,
        (cot_left, cot, cot_right), w_out, conv_weight, conv_bias,
    )

    msg = msg.reshape(pat_dev, lat_dev, width + 128)
    msgs = [msg] + [lax.ppermute(msg, "zh", shift("zh", NZH, s)) for s in range(1, NZH)]
    dq = backward_attention(zh.reshape(1), kv, valid, queries, msgs)

    pieces = lax.all_to_all(dq, ("zh", "tm"), 0, 0, tiled=True)
    dq_row = jnp.sum(pieces, axis=0, keepdims=True).astype(bf16)
    dq_all = lax.all_to_all(
        jnp.broadcast_to(dq_row, (lat_rows, width)), ("y", "zh", "zl", "tm"), 0, 0, tiled=True
    )
    d_latents = nt_dot(dq_all, w_query)
    return features.reshape(pat_dev, lat_dev, width), d_latents


def solution(mesh):
    split = Mesh(mesh.devices.reshape(NY, NZH, NZL, NTM), ("y", "zh", "zl", "tm"))
    contacts = ("y", "zh", "zl")
    in_specs = (
        P(contacts, "tm"),
        P(contacts),
        P(contacts),
        P(),
        P(),
        P(),
        P(),
        P(),
        P(),
        P(),
        P(),
        P("tm", contacts, None),
    )
    out_specs = (P("tm", contacts, None), P())
    return jax.shard_map(local, mesh=split, in_specs=in_specs, out_specs=out_specs, check_vma=False)
```

time: 1140 us -> 169 us (0.15)
  waiting for transfers between devices: 662 us -> 6.6 us
  local copies, waits for them, and re-layouts: 191 us -> 10.1 us
  other arithmetic: 136 us -> 4.07 us
  Pallas kernels: 0 us -> 57.9 us
  blocking collectives: 82.5 us -> 42.6 us
  matrix products: 28.2 us -> 1.93 us
  starting transfers between devices: 22.8 us -> 43.3 us
  between operations: 14.1 us -> 1.59 us
    all_gather x4 -> x0, waiting for transfers between devices: 654 us -> none  [the longest x3 585 us: joined(): everything = jax.tree.map(lambda part: lax.all_gather(part, axis), x)]
    dynamic_slice x76 -> x1, local copies, waits for them, and re-layouts: 160 us -> 0.75 us  [local(): lax.dynamic_index_in_dim(mine, (zh + NZH - s) % NZH, 0, False)]
    add x62 -> x0, other arithmetic: 125 us -> none  [the longest x31 100 us: combine_parts(): split_heads(acc_a, head_count) * fac_a[..., None]]
    psum x1 -> x0, blocking collectives: 82.5 us -> none  [local(): lax.psum((dq_sum * scale_dot).reshape(lat_rows, model_width), ('contacts'...]
    pallas_call x0 -> x5, Pallas kernels: none -> 57.9 us  [the longest x1 24.3 us: forward_attention(): pl.pallas_call(forward_kernel, grid=(windows,), in_specs=[whole(sig), who...]
    all_to_all x0 -> x2, blocking collectives: none -> 42.6 us  [the longest x1 21.4 us: local(): pieces = lax.all_to_all(dq, ('zh', 'tm'), 0, 0, tiled=True)]
    dot_general x17 -> x2, matrix products: 28.2 us -> 1.93 us  [the longest x1 1.13 us: nt_dot(): lax.dot_general(a, b, (((1,), (1,)), ((), ())), preferred_element_type=f32)]
    ppermute x8 -> x16, starting transfers between devices: 22.6 us -> 43.3 us  [the longest x3 9.61 us: local(): lax.ppermute(parts[s], 'zh', shift('zh', NZH, -s))]
  transfers between devices with their start and end apart: 12 -> 16, of which waited for: 8 -> 5; matrix products, arithmetic and copies ran while one was open for 0% -> 1% of each run, Pallas kernels for 0% -> 1%
where the time goes in v1:
time: 169 us; the launch traced here: 168 us
  Pallas kernels  57.9 us (34%)
  starting transfers between devices  43.3 us (26%)
  blocking collectives  42.6 us (25%)
  local copies, waits for them, and re-layouts  10.1 us (6%)
  waiting for transfers between devices  6.6 us (4%)
  other arithmetic  4.07 us (2%)
  matrix products  1.93 us (1%)
    pallas_call x1, Pallas kernels, forward_attention(): pl.pallas_call(forward_kernel, grid=(windows,), in_specs=[whole(sig), who...  24.3 us
    all_to_all x1, blocking collectives, local(): pieces = lax.all_to_all(dq, ('zh', 'tm'), 0, 0, tiled=True)  21.4 us
    all_to_all x1, blocking collectives, local(): lax.all_to_all(jnp.broadcast_to(dq_row, (lat_rows, width)), ('y', 'zh', '...  21.2 us
    pallas_call x1, Pallas kernels, pos_rows(): pl.pallas_call(pos_kernel, grid=(rows // tile,), in_specs=[pl.BlockSpec((...  13.4 us
    pallas_call x1, Pallas kernels, backward_attention(): pl.pallas_call(backward_kernel, grid=(windows,), in_specs=[pl.BlockSpec(m...  13.1 us
    ppermute x3, starting transfers between devices, local(): lax.ppermute(parts[s], 'zh', shift('zh', NZH, -s))  9.61 us
    ppermute x3, starting transfers between devices, local(): lax.ppermute(msg, 'zh', shift('zh', NZH, s))  7.08 us
    ppermute x1, starting transfers between devices, local(): cot_left = lax.ppermute(cot[lat_dev:], 'tm', up1)  6.12 us
  transfers between devices with their start and end apart: 16, of which 5 were waited for; matrix products, arithmetic and copies ran while one was open for 1% of the time, Pallas kernels for 1%

profile of v1, /device:TPU:1, one launch (start us, length us, event | category | flops | bytes accessed | tf_op | source)
XLA Modules:
  0.0 168.2 jit_solution(11353195852509782440)
XLA Ops:
  0.6 0.0 copy-start
  0.6 0.7 fusion.13
  2.1 0.1 pad.9.clone
  2.1 0.9 constant_dynamic-update-slice_fusion.4
  3.1 2.5 %collective-permute-start = (bf16[264,128]{1,0:T(8,128)(2,1)S(1)}, bf16[264,128]{1,0:T(8,128)(2,1)S(1)}, u32[]{:S(2)}, u32[]{:S(2)}) collective-permute-start(bf16[264,128]{1,0:T(8,128)(2,1)S(1)} %get-tuple-element.15), channel_id=1, source_target_pairs={{0,8},{8,0},{1,9},{9,1},{2,10},{10,2},{3,11},{11,3},{4,12},{12,4},... | collective-permute-start | bytes 202760 | tf_op jit(solution)/shard_map/ppermute | solution.py:362
  5.6 0.7 dynamic-slice_bitcast_fusion.3
  6.4 0.8 convolution_convert_fusion.q_ref
  7.2 0.1 collective-permute-done
  7.3 1.4 collective-permute-start.1
  8.7 2.6 %collective-permute-start.2 = (bf16[2,264,128]{2,1,0:T(8,128)(2,1)S(1)}, bf16[2,264,128]{2,1,0:T(8,128)(2,1)S(1)}, u32[]{:S(2)}, u32[]{:S(2)}) collective-permute-start(bf16[2,264,128]{2,1,0:T(8,128)(2,1)S(1)} %pad_maximum_fusion), channel_id=1, source_target_pairs={{0,128},{64,192},{128,0},{192,64},{1,129},{65,193},{129,1},{193,65... | collective-permute-start | bytes 405512 | tf_op jit(solution)/shard_map/ppermute | solution.py:364
  11.3 1.1 collective-permute-start.3
  12.4 0.1 collective-permute-done.1
  12.6 3.4 %collective-permute-done.2 = bf16[2,264,128]{2,1,0:T(8,128)(2,1)S(1)} collective-permute-done((bf16[2,264,128]{2,1,0:T(8,128)(2,1)S(1)}, bf16[2,264,128]{2,1,0:T(8,128)(2,1)S(1)}, u32[]{:S(2)}, u32[]{:S(2)}) %collective-permute-start.2) | collective-permute-done | bytes 135200 | tf_op jit(solution)/shard_map/ppermute | solution.py:364
  16.0 0.0 collective-permute-done.3
  16.0 0.1 slice_reduce_fusion
  16.2 0.8 slice.60
  17.0 0.1 convert_bitcast_fusion
  17.1 0.6 copy.18
  17.7 1.4 copy.15.idx_ref
  19.1 13.4 %pos_rows.1.pos_ref = bf16[2048,512]{1,0:T(8,128)(2,1)} custom-call(s32[2048,1]{1,0:T(8,128)} %copy.15.idx_ref, bf16[4096,512]{1,0:T(8,128)(2,1)} %table_ref.1), custom_call_target="tpu_custom_call" | custom-call | tf_op jit(solution)/shard_map/pos_rows/pallas_call | solution.py:95
  32.4 24.3 %forward_attention.1 = (bf16[4,2048,1024]{2,1,0:T(8,128)(2,1)}, f32[4,4,8,640]{3,2,1,0:T(8,128)}) custom-call(bf16[2048,128]{1,0:T(8,128)(2,1)} %bitcast.50, bf16[2048,512]{1,0:T(8,128)(2,1)} %pos_rows.1.pos_ref, f32[1,2048]{1,0:T(1,128)} %bitcast.55, bf16[32,512]{1,0:T(8,128)(2,1)} %convolution_convert_fusion.q_ref, bf16[32,512]{1,0:T(8,128)(2,1)} %w_in_ref.1, ...), custom_call_target="tpu_custom_call" | custom-call | tf_op jit(solution)/shard_map/forward_attention/pallas_call | solution.py:151
  56.8 1.7 slice_bitcast_fusion
  58.4 6.4 %collective-permute-start.4 = (f32[4,8,640]{2,1,0:T(8,128)S(1)}, f32[4,8,640]{2,1,0:T(8,128)S(1)}, u32[]{:S(2)}, u32[]{:S(2)}) collective-permute-start(f32[4,8,640]{2,1,0:T(8,128)S(1)} %get-tuple-element.18), channel_id=1, source_target_pairs={{0,48},{16,0},{32,16},{48,32},{1,49},{17,1},{33,17},{49,33},{2,50}... | collective-permute-start | bytes 245768 | tf_op jit(solution)/shard_map/ppermute | solution.py:384
  64.8 0.9 collective-permute-start.5
  65.7 2.4 %collective-permute-start.6 = (f32[4,8,640]{2,1,0:T(8,128)S(1)}, f32[4,8,640]{2,1,0:T(8,128)S(1)}, u32[]{:S(2)}, u32[]{:S(2)}) collective-permute-start(f32[4,8,640]{2,1,0:T(8,128)S(1)} %get-tuple-element.16), channel_id=1, source_target_pairs={{0,16},{16,32},{32,48},{48,0},{1,17},{17,33},{33,49},{49,1},{2,18}... | collective-permute-start | bytes 245768 | tf_op jit(solution)/shard_map/ppermute | solution.py:384
  68.0 6.1 %collective-permute-start.11 = (bf16[24,512]{1,0:T(8,128)(2,1)S(1)}, bf16[24,512]{1,0:T(8,128)(2,1)S(1)}, u32[]{:S(2)}, u32[]{:S(2)}) collective-permute-start(bf16[24,512]{1,0:T(8,128)(2,1)S(1)} %get-tuple-element.25), channel_id=1, source_target_pairs={{0,1},{1,2},{2,3},{3,4},{4,5},{5,6},{6,7},{8,9},{9,10},{10,11},{11... | collective-permute-start | bytes 73736 | tf_op jit(solution)/shard_map/ppermute | solution.py:374
  74.2 1.9 %collective-permute-start.12 = (bf16[24,512]{1,0:T(8,128)(2,1)S(1)}, bf16[24,512]{1,0:T(8,128)(2,1)S(1)}, u32[]{:S(2)}, u32[]{:S(2)}) collective-permute-start(bf16[24,512]{1,0:T(8,128)(2,1)S(1)} %get-tuple-element.24), channel_id=1, source_target_pairs={{1,0},{2,1},{3,2},{4,3},{5,4},{6,5},{7,6},{9,8},{10,9},{11,10},{12... | collective-permute-start | bytes 73736 | tf_op jit(solution)/shard_map/ppermute | solution.py:375
  76.1 0.0 collective-permute-done.4.refs_1_
  76.1 0.0 collective-permute-done.5.refs_2_
  76.2 0.6 copy-done.2
  76.7 0.0 copy-done.3
  76.8 0.0 copy-done.4
  76.8 2.0 %combine_parts.1 = (bf16[32,512]{1,0:T(8,128)(2,1)}, f32[32,128]{1,0:T(8,128)}) custom-call(f32[4,8,640]{2,1,0:T(8,128)} %get-tuple-element.19.refs_0_, f32[4,8,640]{2,1,0:T(8,128)} %copy-done.2, f32[4,8,640]{2,1,0:T(8,128)} %copy-done.3, f32[4,8,640]{2,1,0:T(8,128)} %copy-done.4), custom_call_target="tpu_custom_call" | custom-call | tf_op jit(solution)/shard_map/combine_parts/pallas_call | solution.py:191
  78.8 3.6 %collective-permute-start.8 = (bf16[32,512]{1,0:T(8,128)(2,1)}, bf16[32,512]{1,0:T(8,128)(2,1)S(1)}, u32[]{:S(2)}, u32[]{:S(2)}) collective-permute-start(bf16[32,512]{1,0:T(8,128)(2,1)} %get-tuple-element.9.own_ref), channel_id=1, source_target_pairs={{0,1},{1,2},{2,3},{3,4},{4,5},{5,6},{6,7},{8,9},{9,10},{10,11},{11... | collective-permute-start | bytes 98312 | tf_op jit(solution)/shard_map/ppermute | solution.py:387
  82.5 1.9 %collective-permute-start.9 = (bf16[32,512]{1,0:T(8,128)(2,1)}, bf16[32,512]{1,0:T(8,128)(2,1)S(1)}, u32[]{:S(2)}, u32[]{:S(2)}) collective-permute-start(bf16[32,512]{1,0:T(8,128)(2,1)} %get-tuple-element.9.own_ref), channel_id=1, source_target_pairs={{1,0},{2,1},{3,2},{4,3},{5,4},{6,5},{7,6},{9,8},{10,9},{11,10},{12... | collective-permute-start | bytes 98312 | tf_op jit(solution)/shard_map/ppermute | solution.py:388
  84.4 0.7 fusion.15
  85.1 1.3 collective-permute-start.10
  86.4 4.2 %collective-permute-start.7 = (bf16[16,512]{1,0:T(8,128)(2,1)S(1)}, bf16[16,512]{1,0:T(8,128)(2,1)S(1)}, u32[]{:S(2)}, u32[]{:S(2)}) collective-permute-start(bf16[16,512]{1,0:T(8,128)(2,1)S(1)} %get-tuple-element.27), channel_id=1, source_target_pairs={{0,2},{1,3},{2,4},{3,5},{4,6},{5,7},{8,10},{9,11},{10,12},{11,13},... | collective-permute-start | bytes 49160 | tf_op jit(solution)/shard_map/ppermute | solution.py:389
  90.6 0.0 collective-permute-done.12.cr_ref
  90.7 0.6 collective-permute-done.7.l2_ref
  91.3 0.0 collective-permute-done.8.l4_ref
  91.3 0.0 collective-permute-done.9.r4_ref
  91.3 0.5 copy-done.13
  91.9 0.0 copy-done.8
  91.9 5.1 %conv_stack.1 = (bf16[32,512]{1,0:T(8,128)(2,1)}, bf16[32,640]{1,0:T(8,128)(2,1)}) custom-call(s32[1]{0:T(128)} %bitcast.tm_ref, bf16[16,512]{1,0:T(8,128)(2,1)} %copy-done.13, bf16[32,512]{1,0:T(8,128)(2,1)} %copy-done.8, bf16[32,512]{1,0:T(8,128)(2,1)} %get-tuple-element.9.own_ref, bf16[32,512]{1,0:T(8,128)(2,1)} %copy-done.9, bf16[16,512]{1,0:T(8,128)(2,1)} %copy-done.12, ...), custom_call_target="tpu_custom_call" | custom-call | tf_op jit(solution)/shard_map/conv_stack/pallas_call | solution.py:259
  97.0 2.4 %collective-permute-start.13 = (bf16[4,8,640]{2,1,0:T(8,128)(2,1)}, bf16[4,8,640]{2,1,0:T(8,128)(2,1)S(1)}, u32[]{:S(2)}, u32[]{:S(2)}) collective-permute-start(bf16[4,8,640]{2,1,0:T(8,128)(2,1)} %bitcast.57), channel_id=1, source_target_pairs={{0,16},{16,32},{32,48},{48,0},{1,17},{17,33},{33,49},{49,1},{2,18}... | collective-permute-start | bytes 122888 | tf_op jit(solution)/shard_map/ppermute | solution.py:397
  99.4 1.3 collective-permute-start.14
  100.8 3.3 %collective-permute-start.15 = (bf16[4,8,640]{2,1,0:T(8,128)(2,1)}, bf16[4,8,640]{2,1,0:T(8,128)(2,1)S(1)}, u32[]{:S(2)}, u32[]{:S(2)}) collective-permute-start(bf16[4,8,640]{2,1,0:T(8,128)(2,1)} %bitcast.59), channel_id=1, source_target_pairs={{0,48},{16,0},{32,16},{48,32},{1,49},{17,1},{33,17},{49,33},{2,50}... | collective-permute-start | bytes 122888 | tf_op jit(solution)/shard_map/ppermute | solution.py:397
  104.1 0.0 collective-permute-done.13.refs_1_
  104.1 2.3 %collective-permute-done.14.refs_2_ = bf16[4,8,640]{2,1,0:T(8,128)(2,1)S(1)} collective-permute-done((bf16[4,8,640]{2,1,0:T(8,128)(2,1)}, bf16[4,8,640]{2,1,0:T(8,128)(2,1)S(1)}, u32[]{:S(2)}, u32[]{:S(2)}) %collective-permute-start.14) | collective-permute-done | bytes 40992 | tf_op jit(solution)/shard_map/ppermute | solution.py:397
  106.4 0.0 collective-permute-done.15.refs_3_
  106.4 0.6 copy-done.6
  107.0 0.0 copy-done.7
  107.0 13.1 %backward_attention.1 = f32[32,512]{1,0:T(8,128)} custom-call(s32[1]{0:T(128)} %bitcast.22.zh_ref, bf16[4,2048,1024]{2,1,0:T(8,128)(2,1)} %get-tuple-element.12.kv_ref, f32[1,2048]{1,0:T(1,128)} %bitcast.56, bf16[32,512]{1,0:T(8,128)(2,1)} %convolution_convert_fusion.q_ref, bf16[4,8,640]{2,1,0:T(8,128)(2,1)} %bitcast.60, bf16[4,8,640]{2,1,0:T(8,128)(2,1)} %copy-done.5, ...), custom_call_target="tpu_custom_call" | custom-call | tf_op jit(solution)/shard_map/backward_attention/pallas_call | solution.py:320
  120.2 0.9 copy.16
  121.1 21.4 %all_to_all.18 = f32[32,1,512]{2,1,0:T(1,128)S(1)} all-to-all(f32[32,1,512]{2,1,0:T(1,128)S(1)} %copy.16), channel_id=1, replica_groups=mesh['y'=4,'zh'=4,'zl'=2,'tm'=8] {'zh','tm'}, dimensions={0} | all-to-all | bytes 131072 | tf_op jit(solution)/shard_map/all_to_all | solution.py:400
  142.5 0.1 reduce_sum.9
  142.5 0.3 broadcast_in_dim.8
  142.8 0.5 broadcast.60
  143.3 2.2 %reduce.3 = bf16[256,512]{1,0:T(8,128)(2,1)S(1)} reduce(bf16[256,1,512]{2,1,0:T(2,128)(2,1)S(1)} %broadcast_in_dim.8, bf16[]{:T(256)} %broadcast.60), dimensions={1}, to_apply=%broadcast_in_dim.8.reduce_sub_computation | reduce | bytes 524290 | tf_op jit(solution)/shard_map/broadcast_in_dim | solution.py:403
  145.5 0.1 reshape.104
  145.6 21.2 %all_to_all.19 = bf16[256,2,256]{2,1,0:T(2,128)(2,1)S(1)} all-to-all(bf16[256,2,256]{2,1,0:T(2,128)(2,1)S(1)} %reshape.104), channel_id=1, replica_groups=mesh['y'=4,'zh'=4,'zl'=2,'tm'=8] {'y','zh','zl','tm'}, dimensions={0} | all-to-all | bytes 524288 | tf_op jit(solution)/shard_map/all_to_all | solution.py:402
  166.8 0.2 reshape.105
  167.0 1.1 fusion
  (33 shorter events, 0.2 us)
Async XLA Ops:
  0.6 5.7 %copy-start = (bf16[512,512]{1,0:T(8,128)(2,1)S(1)}, bf16[512,512]{1,0:T(8,128)(2,1)}, u32[]{:S(2)}) copy-start(bf16[512,512]{1,0:T(8,128)(2,1)} %param.19) | copy-start | bytes 1572868
  3.1 4.2 %collective-permute-start = (bf16[264,128]{1,0:T(8,128)(2,1)S(1)}, bf16[264,128]{1,0:T(8,128)(2,1)S(1)}, u32[]{:S(2)}, u32[]{:S(2)}) collective-permute-start(bf16[264,128]{1,0:T(8,128)(2,1)S(1)} %get-tuple-element.15), channel_id=1, source_target_pairs={{0,8},{8,0},{1,9},{9,1},{2,10},{10,2},{3,11},{11,3},{4,12},{12,4},... | collective-permute-start | bytes 202760 | tf_op jit(solution)/shard_map/ppermute | solution.py:362
  7.3 5.2 %collective-permute-start.1 = (bf16[2,264,128]{2,1,0:T(8,128)(2,1)S(1)}, bf16[2,264,128]{2,1,0:T(8,128)(2,1)S(1)}, u32[]{:S(2)}, u32[]{:S(2)}) collective-permute-start(bf16[2,264,128]{2,1,0:T(8,128)(2,1)S(1)} %pad_maximum_fusion), channel_id=1, source_target_pairs={{0,64},{64,128},{128,192},{192,0},{1,65},{65,129},{129,193},{193,1... | collective-permute-start | bytes 405512 | tf_op jit(solution)/shard_map/ppermute | solution.py:364
  8.7 7.3 %collective-permute-start.2 = (bf16[2,264,128]{2,1,0:T(8,128)(2,1)S(1)}, bf16[2,264,128]{2,1,0:T(8,128)(2,1)S(1)}, u32[]{:S(2)}, u32[]{:S(2)}) collective-permute-start(bf16[2,264,128]{2,1,0:T(8,128)(2,1)S(1)} %pad_maximum_fusion), channel_id=1, source_target_pairs={{0,128},{64,192},{128,0},{192,64},{1,129},{65,193},{129,1},{193,65... | collective-permute-start | bytes 405512 | tf_op jit(solution)/shard_map/ppermute | solution.py:364
  11.3 4.7 %collective-permute-start.3 = (bf16[2,264,128]{2,1,0:T(8,128)(2,1)S(1)}, bf16[2,264,128]{2,1,0:T(8,128)(2,1)S(1)}, u32[]{:S(2)}, u32[]{:S(2)}) collective-permute-start(bf16[2,264,128]{2,1,0:T(8,128)(2,1)S(1)} %pad_maximum_fusion), channel_id=1, source_target_pairs={{0,192},{64,0},{128,64},{192,128},{1,193},{65,1},{129,65},{193,129... | collective-permute-start | bytes 405512 | tf_op jit(solution)/shard_map/ppermute | solution.py:364
  19.1 49.0 %copy-start.1 = (bf16[4,8,512]{2,1,0:T(8,128)(2,1)S(1)}, bf16[4,8,512]{2,1,0:T(8,128)(2,1)}, u32[]{:S(2)}) copy-start(bf16[4,8,512]{2,1,0:T(8,128)(2,1)} %param.23) | copy-start | bytes 98308
  58.4 17.7 %collective-permute-start.4 = (f32[4,8,640]{2,1,0:T(8,128)S(1)}, f32[4,8,640]{2,1,0:T(8,128)S(1)}, u32[]{:S(2)}, u32[]{:S(2)}) collective-permute-start(f32[4,8,640]{2,1,0:T(8,128)S(1)} %get-tuple-element.18), channel_id=1, source_target_pairs={{0,48},{16,0},{32,16},{48,32},{1,49},{17,1},{33,17},{49,33},{2,50}... | collective-permute-start | bytes 245768 | tf_op jit(solution)/shard_map/ppermute | solution.py:384
  64.8 11.3 %collective-permute-start.5 = (f32[4,8,640]{2,1,0:T(8,128)S(1)}, f32[4,8,640]{2,1,0:T(8,128)S(1)}, u32[]{:S(2)}, u32[]{:S(2)}) collective-permute-start(f32[4,8,640]{2,1,0:T(8,128)S(1)} %get-tuple-element.17), channel_id=1, source_target_pairs={{0,32},{16,48},{32,0},{48,16},{1,33},{17,49},{33,1},{49,17},{2,34}... | collective-permute-start | bytes 245768 | tf_op jit(solution)/shard_map/ppermute | solution.py:384
  65.7 10.5 %collective-permute-start.6 = (f32[4,8,640]{2,1,0:T(8,128)S(1)}, f32[4,8,640]{2,1,0:T(8,128)S(1)}, u32[]{:S(2)}, u32[]{:S(2)}) collective-permute-start(f32[4,8,640]{2,1,0:T(8,128)S(1)} %get-tuple-element.16), channel_id=1, source_target_pairs={{0,16},{16,32},{32,48},{48,0},{1,17},{17,33},{33,49},{49,1},{2,18}... | collective-permute-start | bytes 245768 | tf_op jit(solution)/shard_map/ppermute | solution.py:384
  68.0 18.4 %collective-permute-start.11 = (bf16[24,512]{1,0:T(8,128)(2,1)S(1)}, bf16[24,512]{1,0:T(8,128)(2,1)S(1)}, u32[]{:S(2)}, u32[]{:S(2)}) collective-permute-start(bf16[24,512]{1,0:T(8,128)(2,1)S(1)} %get-tuple-element.25), channel_id=1, source_target_pairs={{0,1},{1,2},{2,3},{3,4},{4,5},{5,6},{6,7},{8,9},{9,10},{10,11},{11... | collective-permute-start | bytes 73736 | tf_op jit(solution)/shard_map/ppermute | solution.py:374
  74.2 16.5 %collective-permute-start.12 = (bf16[24,512]{1,0:T(8,128)(2,1)S(1)}, bf16[24,512]{1,0:T(8,128)(2,1)S(1)}, u32[]{:S(2)}, u32[]{:S(2)}) collective-permute-start(bf16[24,512]{1,0:T(8,128)(2,1)S(1)} %get-tuple-element.24), channel_id=1, source_target_pairs={{1,0},{2,1},{3,2},{4,3},{5,4},{6,5},{7,6},{9,8},{10,9},{11,10},{12... | collective-permute-start | bytes 73736 | tf_op jit(solution)/shard_map/ppermute | solution.py:375
  76.1 0.6 copy-start.2
  76.1 0.7 copy-start.3
  76.1 0.7 copy-start.4
  78.8 12.5 %collective-permute-start.8 = (bf16[32,512]{1,0:T(8,128)(2,1)}, bf16[32,512]{1,0:T(8,128)(2,1)S(1)}, u32[]{:S(2)}, u32[]{:S(2)}) collective-permute-start(bf16[32,512]{1,0:T(8,128)(2,1)} %get-tuple-element.9.own_ref), channel_id=1, source_target_pairs={{0,1},{1,2},{2,3},{3,4},{4,5},{5,6},{6,7},{8,9},{9,10},{10,11},{11... | collective-permute-start | bytes 98312 | tf_op jit(solution)/shard_map/ppermute | solution.py:387
  82.5 8.8 %collective-permute-start.9 = (bf16[32,512]{1,0:T(8,128)(2,1)}, bf16[32,512]{1,0:T(8,128)(2,1)S(1)}, u32[]{:S(2)}, u32[]{:S(2)}) collective-permute-start(bf16[32,512]{1,0:T(8,128)(2,1)} %get-tuple-element.9.own_ref), channel_id=1, source_target_pairs={{1,0},{2,1},{3,2},{4,3},{5,4},{6,5},{7,6},{9,8},{10,9},{11,10},{12... | collective-permute-start | bytes 98312 | tf_op jit(solution)/shard_map/ppermute | solution.py:388
  85.1 5.5 %collective-permute-start.10 = (bf16[16,512]{1,0:T(8,128)(2,1)S(1)}, bf16[16,512]{1,0:T(8,128)(2,1)S(1)}, u32[]{:S(2)}, u32[]{:S(2)}) collective-permute-start(bf16[16,512]{1,0:T(8,128)(2,1)S(1)} %get-tuple-element.26), channel_id=1, source_target_pairs={{2,0},{3,1},{4,2},{5,3},{6,4},{7,5},{10,8},{11,9},{12,10},{13,11},... | collective-permute-start | bytes 49160 | tf_op jit(solution)/shard_map/ppermute | solution.py:390
  86.4 4.9 %copy-start.10 = (bf16[24,512]{1,0:T(8,128)(2,1)}, bf16[24,512]{1,0:T(8,128)(2,1)S(1)}, u32[]{:S(2)}) copy-start(bf16[24,512]{1,0:T(8,128)(2,1)S(1)} %collective-permute-done.11.cl_ref) | copy-start | bytes 73732
  86.4 4.8 %collective-permute-start.7 = (bf16[16,512]{1,0:T(8,128)(2,1)S(1)}, bf16[16,512]{1,0:T(8,128)(2,1)S(1)}, u32[]{:S(2)}, u32[]{:S(2)}) collective-permute-start(bf16[16,512]{1,0:T(8,128)(2,1)S(1)} %get-tuple-element.27), channel_id=1, source_target_pairs={{0,2},{1,3},{2,4},{3,5},{4,6},{5,7},{8,10},{9,11},{10,12},{11,13},... | collective-permute-start | bytes 49160 | tf_op jit(solution)/shard_map/ppermute | solution.py:389
  90.6 0.7 copy-start.11
  90.6 0.7 copy-start.12
  91.3 0.6 copy-start.13
  91.3 0.6 copy-start.8
  91.3 0.6 copy-start.9
  97.0 7.1 %collective-permute-start.13 = (bf16[4,8,640]{2,1,0:T(8,128)(2,1)}, bf16[4,8,640]{2,1,0:T(8,128)(2,1)S(1)}, u32[]{:S(2)}, u32[]{:S(2)}) collective-permute-start(bf16[4,8,640]{2,1,0:T(8,128)(2,1)} %bitcast.57), channel_id=1, source_target_pairs={{0,16},{16,32},{32,48},{48,0},{1,17},{17,33},{33,49},{49,1},{2,18}... | collective-permute-start | bytes 122888 | tf_op jit(solution)/shard_map/ppermute | solution.py:397
  99.4 7.0 %collective-permute-start.14 = (bf16[4,8,640]{2,1,0:T(8,128)(2,1)}, bf16[4,8,640]{2,1,0:T(8,128)(2,1)S(1)}, u32[]{:S(2)}, u32[]{:S(2)}) collective-permute-start(bf16[4,8,640]{2,1,0:T(8,128)(2,1)} %bitcast.58), channel_id=1, source_target_pairs={{0,32},{16,48},{32,0},{48,16},{1,33},{17,49},{33,1},{49,17},{2,34}... | collective-permute-start | bytes 122888 | tf_op jit(solution)/shard_map/ppermute | solution.py:397
  100.8 5.7 %collective-permute-start.15 = (bf16[4,8,640]{2,1,0:T(8,128)(2,1)}, bf16[4,8,640]{2,1,0:T(8,128)(2,1)S(1)}, u32[]{:S(2)}, u32[]{:S(2)}) collective-permute-start(bf16[4,8,640]{2,1,0:T(8,128)(2,1)} %bitcast.59), channel_id=1, source_target_pairs={{0,48},{16,0},{32,16},{48,32},{1,49},{17,1},{33,17},{49,33},{2,50}... | collective-permute-start | bytes 122888 | tf_op jit(solution)/shard_map/ppermute | solution.py:397
  104.1 2.3 %copy-start.5 = (bf16[4,8,640]{2,1,0:T(8,128)(2,1)}, bf16[4,8,640]{2,1,0:T(8,128)(2,1)S(1)}, u32[]{:S(2)}) copy-start(bf16[4,8,640]{2,1,0:T(8,128)(2,1)S(1)} %collective-permute-done.13.refs_1_) | copy-start | bytes 122884
  106.4 0.6 copy-start.6
  106.4 0.6 copy-start.7

commit v2 on v1

v2 whole, which is shorter than its diff:
```python
import functools

import jax
import jax.numpy as jnp
from jax import lax
from jax.experimental import pallas as pl
from jax.experimental.pallas import tpu as pltpu
from jax.sharding import Mesh
from jax.sharding import PartitionSpec as P

HD = 64
PATCH = 32
KSIZE = 3
LAYERS = 2

neg_big = -1e30
scale_dot = 0.125

bf16 = jnp.bfloat16
f32 = jnp.float32

NY, NZ, NTM = 4, 8, 8
MIB = 1 << 20


def nt_dot(a, b):
    return lax.dot_general(a, b, (((1,), (1,)), ((), ())), preferred_element_type=f32)


def nn_dot(a, b):
    return jnp.dot(a, b, preferred_element_type=f32)


def head_of_lane(shape):
    return lax.broadcasted_iota(jnp.int32, shape, len(shape) - 1) // HD


def spread_heads(rows, heads):
    head = head_of_lane(rows.shape)
    zero = jnp.zeros_like(rows)
    return jnp.concatenate([jnp.where(head == h, rows, zero) for h in range(heads)], axis=0)


def collect_heads(blocks, heads):
    r = blocks.shape[0] // heads
    head = head_of_lane((r, blocks.shape[1]))
    out = blocks[:r]
    for h in range(1, heads):
        out = jnp.where(head == h, blocks[h * r : (h + 1) * r], out)
    return out


def columns_to_lanes(column, heads, first, base):
    r = base.shape[0]
    lane = lax.broadcasted_iota(jnp.int32, base.shape, 1)
    for h in range(heads):
        base = jnp.where(lane == first + h, column[h * r : (h + 1) * r], base)
    return base


def lanes_to_column(stats, heads, first):
    return jnp.concatenate([stats[:, first + h : first + h + 1] for h in range(heads)], axis=0)


def lanes_to_columns_wide(stats, heads, first):
    r = stats.shape[0]
    head = head_of_lane((r, heads * HD))
    out = jnp.broadcast_to(stats[:, first : first + 1], (r, heads * HD))
    for h in range(1, heads):
        out = jnp.where(head == h, stats[:, first + h : first + h + 1], out)
    return out


def silu_slope(pre_act):
    sigmoid_v = jax.nn.sigmoid(pre_act)
    return sigmoid_v * (1.0 + pre_act * (1.0 - sigmoid_v))


def rounded(value):
    return value.astype(bf16).astype(f32)


def absorb_kernel(*refs, fresh, last, count):
    refs = list(refs)
    messages = [refs.pop(0) for _ in range(count)]
    q_ref, w_in_ref, w_kv_ref, table_ref = (refs.pop(0) for _ in range(4))
    if not fresh:
        refs.pop(0), refs.pop(0)
        acc_in, stat_in = refs.pop(0), refs.pop(0)
    kv_ref, valid_ref = refs.pop(0), refs.pop(0)
    if last:
        part_refs = [refs.pop(0) for _ in range(NY)]
    else:
        acc_out, stat_out = refs.pop(0), refs.pop(0)
    pos_ref = refs.pop(0)
    width = q_ref.shape[1]
    heads = width // HD
    con_dev, span = messages[0].shape[0], messages[0].shape[1] - 128
    step_no = pl.program_id(0)
    message = messages[0][...]
    if count == 2:
        message = jnp.where(step_no == 0, message, messages[1][...])
    sig = message[:, :span]
    meta = message[:, span:].astype(f32)
    idx = meta[:, 0:1] * 64.0 + meta[:, 1:2]
    live = meta[0:1, 2:3]
    lane = lax.broadcasted_iota(jnp.int32, (1, con_dev), 1).astype(f32)
    valid = jnp.where(lane < live, 1.0, 0.0)
    valid_ref[...] = jnp.broadcast_to(valid, valid_ref.shape)
    piece = 512
    ids = lax.broadcasted_iota(jnp.int32, (con_dev, piece), 1).astype(f32)

    def add_rows(k, pos):
        for part in range(2):
            start = pl.multiple_of((2 * k + part) * piece, piece)
            hot = jnp.where(ids == idx - start.astype(f32), 1.0, 0.0).astype(bf16)
            pos = pos + nn_dot(hot, table_ref[pl.ds(start, piece), :])
        return pos

    pos = lax.fori_loop(0, table_ref.shape[0] // (2 * piece), add_rows, jnp.zeros((con_dev, width), f32))
    pos_ref[...] = pos
    windows = span // PATCH

    def one_window(w):
        pos = pos_ref[...]
        q_wide = spread_heads(q_ref[...], heads)
        tall = jnp.concatenate([w_in_ref[...]] * windows, axis=0)
        band = lax.broadcasted_iota(jnp.int32, tall.shape, 0) // PATCH
        embedded = nn_dot(sig, jnp.where(band == w, tall, jnp.zeros_like(tall)))
        tokens = (embedded + pos).astype(bf16)
        keyval = nn_dot(tokens, w_kv_ref[...]).astype(bf16)
        kv_ref[w] = keyval
        scores = nt_dot(q_wide, keyval[:, :width]) * scale_dot
        scores = jnp.where(valid > 0.0, scores, neg_big)
        top = jnp.max(scores, axis=1, keepdims=True)
        if not fresh:
            acc_now, stat_now = (acc_out, stat_out) if count > 1 else (acc_in, stat_in)
            before, total_before, acc_before = stat_now[w, :, 0:1], stat_now[w, :, 1:2], acc_now[w]
            top = jnp.maximum(top, before)
        weights = jnp.exp(scores - top)
        totals = jnp.sum(weights, axis=1, keepdims=True)
        accum = nn_dot(weights.astype(bf16), keyval[:, width:])
        if not fresh:
            fade = jnp.exp(before - top)
            totals = totals + total_before * fade
            accum = accum + acc_before * fade
        if not last:
            acc_out[w] = accum
            stat_out[w, :, 0:1] = top
            stat_out[w, :, 1:2] = totals
        else:
            mixed = collect_heads(accum, heads)
            stats = jnp.zeros((mixed.shape[0], 128), f32)
            stats = columns_to_lanes(top, heads, 0, stats)
            stats = columns_to_lanes(totals, heads, heads, stats)
            each = mixed.shape[0] // NY
            for s, part_ref in enumerate(part_refs):
                part_ref[w, :, :width] = mixed[s * each : (s + 1) * each]
                part_ref[w, :, width:] = stats[s * each : (s + 1) * each]

    if count > 1:

        @pl.when(step_no == 0)
        def _():
            acc_out[...] = acc_in[...]
            stat_out[...] = stat_in[...]

    @pl.loop(0, windows // 2)
    def _(k):
        one_window(2 * k)
        one_window(2 * k + 1)


def absorb(messages, base, q, w_in, w_kv, table, state, last):
    count = len(messages)
    lat, width = q.shape
    con_dev = messages[0].shape[0]
    windows = (messages[0].shape[1] - 128) // PATCH
    rows = lat * (width // HD)
    fresh = state is None
    whole = lambda a: pl.BlockSpec(a.shape, lambda i: (0,) * a.ndim, pipeline_mode=pl.Buffered(1))
    fixed = lambda shape: pl.BlockSpec(shape, lambda i: (0,) * len(shape), pipeline_mode=pl.Buffered(1))
    anywhere = pl.BlockSpec(memory_space=pl.ANY)
    operands = list(messages) + [q, w_in, w_kv, table]
    in_specs = [whole(a) for a in operands]
    aliases = {}
    if not fresh:
        n = len(operands)
        operands += list(state)
        in_specs += [anywhere, anywhere] + [whole(a) for a in state[2:]]
        aliases = {n: 0, n + 1: 1}
    acc = jax.ShapeDtypeStruct((windows, rows, width), f32)
    stat = jax.ShapeDtypeStruct((windows, rows, 128), f32)
    part = jax.ShapeDtypeStruct((windows, lat // NY, width + 128), f32)
    tail = [part] * NY if last else [acc, stat]
    return pl.pallas_call(
        functools.partial(absorb_kernel, fresh=fresh, last=last, count=count),
        grid=(count,),
        in_specs=in_specs,
        out_specs=[
            pl.BlockSpec((windows, con_dev, 2 * width), lambda i: (0, base + i, 0)),
            pl.BlockSpec((8, con_dev), lambda i: (0, base + i)),
        ]
        + [fixed(a.shape) for a in tail],
        out_shape=[
            jax.ShapeDtypeStruct((windows, NZ * con_dev, 2 * width), bf16),
            jax.ShapeDtypeStruct((8, NZ * con_dev), f32),
        ]
        + tail,
        scratch_shapes=[pltpu.VMEM((con_dev, width), f32)],
        input_output_aliases=aliases,
        compiler_params=pltpu.CompilerParams(vmem_limit_bytes=28 * MIB),
        name="absorb",
    )(*operands)


def combine_kernel(*refs):
    *part_refs, att_ref, stats_ref = refs
    rows, width = att_ref.shape
    heads = width // HD
    lane = lax.broadcasted_iota(jnp.int32, (rows, 128), 1)
    parts = [ref[...].reshape(rows, width + 128) for ref in part_refs]
    top = parts[0][:, width:]
    for part in parts[1:]:
        top = jnp.maximum(top, part[:, width:])
    totals = jnp.zeros((rows, 128), f32)
    accum = jnp.zeros((rows, width), f32)
    for part in parts:
        factor = jnp.exp(jnp.where(lane < heads, part[:, width:] - top, 0.0))
        totals = totals + factor * pltpu.roll(part[:, width:], 128 - heads, 1)
        accum = accum + part[:, :width] * lanes_to_columns_wide(factor, heads, 0)
    totals = jnp.where(lane < heads, totals, 1.0)
    att_ref[...] = (accum / lanes_to_columns_wide(totals, heads, 0)).astype(bf16)
    stats_ref[...] = jnp.where(lane < heads, top, pltpu.roll(1.0 / totals, heads, 1))


def combine(parts):
    windows, each, wide = parts[0].shape
    rows = windows * each
    return pl.pallas_call(
        combine_kernel,
        out_shape=[
            jax.ShapeDtypeStruct((rows, wide - 128), bf16),
            jax.ShapeDtypeStruct((rows, 128), f32),
        ],
        compiler_params=pltpu.CompilerParams(vmem_limit_bytes=8 * MIB),
        name="combine_parts",
    )(*parts)


def conv_kernel(
    tm_ref, left_ref, own_ref, partner_ref, right_ref, stats_ref, cl_ref, cot_ref, cr_ref,
    w_out_ref, conv_ref, bias_ref, feat_ref, msg_ref, ext_ref,
):
    rows, width = own_ref.shape
    heads = width // HD
    windows = 4
    each = rows // windows
    reach = 6
    first = tm_ref[0] * windows - reach
    total_windows = NTM * windows

    def inside(lo, count):
        w = lax.broadcasted_iota(jnp.int32, (count * each, width), 0) // each + (first + lo)
        return jnp.logical_and(w >= 0, w < total_windows)

    core = tm_ref[0] % 2
    side = reach * each
    ext_ref[:side, :] = left_ref[...].astype(f32)
    ext_ref[pl.ds(pl.multiple_of(side + core * rows, each), rows), :] = own_ref[...].astype(f32)
    ext_ref[pl.ds(pl.multiple_of(side + (1 - core) * rows, each), rows), :] = partner_ref[...].astype(f32)
    ext_ref[side + 2 * rows :, :] = right_ref[...].astype(f32)
    att = ext_ref[pl.ds(pl.multiple_of(core * rows, each), 2 * side + rows), :]
    w_out = w_out_ref[...]
    x0 = rounded(nn_dot(att.astype(bf16), w_out))
    n0 = 14 * each
    pre0 = bias_ref[0:1, :] + sum(nn_dot(x0[j * each : j * each + n0].astype(bf16), conv_ref[0, j]) for j in range(KSIZE))
    x1 = rounded(x0[each : each + n0] + jax.nn.silu(pre0))
    x1 = jnp.where(inside(1, 14), x1, 0.0)
    n1 = 10 * each
    pre1 = bias_ref[1:2, :] + sum(nn_dot(x1[2 * j * each : 2 * j * each + n1].astype(bf16), conv_ref[1, j]) for j in range(KSIZE))
    feat_ref[...] = (x1[5 * each : 9 * each] + jax.nn.silu(pre1[3 * each : 7 * each])).astype(bf16)
    g2 = jnp.concatenate([r[...].astype(f32) for r in (cl_ref, cot_ref, cr_ref)], axis=0)
    gpre1 = rounded(g2 * silu_slope(pre1))
    n2 = 6 * each
    g1 = g2[2 * each : 8 * each] + sum(
        nt_dot(gpre1[(4 - 2 * j) * each : (4 - 2 * j) * each + n2].astype(bf16), conv_ref[1, j]) for j in range(KSIZE)
    )
    gpre0 = rounded(g1 * silu_slope(pre0[4 * each : 10 * each]))
    gpre0 = jnp.where(inside(5, 6), gpre0, 0.0)
    g0 = g1[each : 5 * each] + sum(
        nt_dot(gpre0[(2 - j) * each : (2 - j) * each + rows].astype(bf16), conv_ref[0, j]) for j in range(KSIZE)
    )
    grad_att = rounded(nt_dot(g0.astype(bf16), w_out))
    msg_ref[:, :width] = grad_att.astype(bf16)
    product = grad_att * own_ref[...].astype(f32)
    head = head_of_lane((rows, width))
    lane = lax.broadcasted_iota(jnp.int32, (rows, 128), 1)
    stats = stats_ref[...]
    for h in range(heads):
        delta = jnp.sum(jnp.where(head == h, product, 0.0), axis=1, keepdims=True)
        stats = jnp.where(lane == 2 * heads + h, delta, stats)
    stats = jnp.where(lane < 3 * heads, stats, 0.0)
    high = rounded(stats)
    middle = rounded(stats - high)
    low = (stats - high) - middle
    msg_ref[:, width:] = (high + pltpu.roll(middle, 32, 1) + pltpu.roll(low, 64, 1)).astype(bf16)


def conv_stack(tm, halo, own, stats, cots, w_out, conv_weight, conv_bias):
    rows, width = own.shape
    left, partner, right = halo
    cl, cot, cr = cots
    vmem = pl.BlockSpec(memory_space=pltpu.VMEM)
    return pl.pallas_call(
        conv_kernel,
        in_specs=[pl.BlockSpec(memory_space=pltpu.SMEM)] + [vmem] * 11,
        out_specs=[vmem, vmem],
        out_shape=[
            jax.ShapeDtypeStruct((rows, width), bf16),
            jax.ShapeDtypeStruct((rows, width + 128), bf16),
        ],
        scratch_shapes=[pltpu.VMEM((left.shape[0] + 2 * rows + right.shape[0], width), f32)],
        compiler_params=pltpu.CompilerParams(vmem_limit_bytes=24 * MIB),
        name="conv_stack",
    )(tm, left, own, partner, right, stats, cl, cot, cr, w_out, conv_weight, conv_bias)


def backward_kernel(y_ref, kv_ref, valid_ref, q_ref, *refs):
    *msg_refs, dq_ref, acc_ref = refs
    width = q_ref.shape[1]
    heads = width // HD
    contacts = kv_ref.shape[1]
    step = 256
    window = pl.program_id(0)
    msg = jnp.concatenate([r[0].astype(f32) for r in msg_refs], axis=0)
    terms = msg[:, width:]
    stats = terms + pltpu.roll(terms, 96, 1) + pltpu.roll(terms, 64, 1)
    top = lanes_to_column(stats, heads, 0)
    inverse = lanes_to_column(stats, heads, heads)
    delta = lanes_to_column(stats, heads, 2 * heads)
    grad_wide = spread_heads(msg[:, :width].astype(bf16), heads)
    q_wide = spread_heads(q_ref[...], heads)

    @pl.when(window == 0)
    def _():
        acc_ref[...] = jnp.zeros_like(acc_ref)

    def one_chunk(start):
        rows = pl.ds(pl.multiple_of(start, step), step)
        key_rows = kv_ref[0, rows, :width]
        scores = nt_dot(q_wide, key_rows) * scale_dot
        scores = jnp.where(valid_ref[0:1, rows] > 0.0, scores, neg_big)
        prob = jnp.exp(scores - top) * inverse
        grad_prob = nt_dot(grad_wide, kv_ref[0, rows, width:])
        dscore = (prob * (grad_prob - delta)).astype(bf16)
        acc_ref[...] = acc_ref[...] + nn_dot(dscore, key_rows)

    @pl.loop(0, contacts // step // 2)
    def _(k):
        one_chunk(2 * k * step)
        one_chunk((2 * k + 1) * step)

    @pl.when(window == pl.num_programs(0) - 1)
    def _():
        dq = collect_heads(acc_ref[...], heads) * scale_dot
        slots = len(msg_refs)
        each = dq.shape[0] // slots
        for s in range(slots):
            place = pl.multiple_of(((y_ref[0] + (slots - s)) % slots) * each, each)
            dq_ref[pl.ds(place, each), :] = dq[s * each : (s + 1) * each]


def backward_attention(y, kv, valid, q, msgs):
    windows, contacts, wide = kv.shape
    lat, width = q.shape
    heads = width // HD
    whole = lambda a: pl.BlockSpec(a.shape, lambda p: (0,) * a.ndim, pipeline_mode=pl.Buffered(1))
    return pl.pallas_call(
        backward_kernel,
        grid=(windows,),
        in_specs=[
            pl.BlockSpec(memory_space=pltpu.SMEM),
            pl.BlockSpec((1, contacts, wide), lambda p: (p, 0, 0)),
            whole(valid),
            whole(q),
        ]
        + [pl.BlockSpec((1,) + m.shape[1:], lambda p: (p, 0, 0)) for m in msgs],
        out_specs=pl.BlockSpec((lat, width), lambda p: (0, 0)),
        out_shape=jax.ShapeDtypeStruct((lat, width), f32),
        scratch_shapes=[pltpu.VMEM((lat * heads, width), f32)],
        compiler_params=pltpu.CompilerParams(vmem_limit_bytes=52 * MIB),
        name="backward_attention",
    )(y, kv, valid, q, *msgs)


def shift(count, by):
    return [(i, (i + by) % count) for i in range(count)]


def local(
    signal, pos_idx, live_count, latents, pos_table, w_in, w_kv, w_query, w_out,
    conv_weight, conv_bias, cotangent,
):
    con_dev = signal.shape[0]
    pat_dev = signal.shape[1] // PATCH
    width = w_query.shape[0]
    lat_rows = latents.shape[0]
    y, z, tm = (lax.axis_index(a) for a in ("y", "z", "tm"))
    lat_dev = lat_rows // (NY * NZ)
    up1 = [(i, i + 1) for i in range(NTM - 1)]
    down1 = [(i + 1, i) for i in range(NTM - 1)]
    up2 = [(i, i + 2) for i in range(NTM - 2)]
    down2 = [(i + 2, i) for i in range(NTM - 2)]
    swap = [(i, i ^ 1) for i in range(NTM)]

    by_owner = latents.reshape(NY, NZ, lat_dev, width)
    mine = lax.dynamic_index_in_dim(by_owner, z, 1, False)
    slots = jnp.stack([lax.dynamic_index_in_dim(mine, (y + NY - s) % NY, 0, False) for s in range(NY)])
    queries = nn_dot(slots.reshape(NY * lat_dev, width), w_query).astype(bf16)

    lane = lax.broadcasted_iota(jnp.int32, (con_dev, 128), 1)
    index = pos_idx[:, None]
    meta = jnp.where(lane == 0, index // 64, jnp.where(lane == 1, index % 64, live_count[0]))
    own = jnp.concatenate([signal, meta.astype(bf16)], axis=1)

    def absorbed(messages, base, state, last=False):
        return absorb(messages, base, queries, w_in, w_kv, pos_table, state, last)

    cot = cotangent.reshape(pat_dev * lat_dev, width)
    cot_left = lax.ppermute(cot[lat_dev:], "tm", up1)
    cot_right = lax.ppermute(cot[: 3 * lat_dev], "tm", down1)

    below, above = own, own
    at_hand, base, state = [own], 0, None
    for step in range(1, NZ // 2 + 1):
        below = lax.ppermute(below, "z", shift(NZ, 1))
        if step < NZ // 2:
            above = lax.ppermute(above, "z", shift(NZ, -1))
        state = list(absorbed(at_hand, base, state))
        base += len(at_hand)
        if step == 2:
            below, above, state[1], cot_left, cot_right = lax.optimization_barrier(
                (below, above, state[1], cot_left, cot_right)
            )
        elif step < NZ // 2:
            below, above, state[1] = lax.optimization_barrier((below, above, state[1]))
        at_hand = [below, above] if step < NZ // 2 else [below]
    kv, valid, *parts = absorbed(at_hand, base, state, last=True)

    received = [lax.ppermute(parts[s], "y", shift(NY, -s)) for s in range(1, NY)]
    att, stats = combine([parts[0]] + received)

    partner = lax.ppermute(att, "tm", swap)
    chip = jnp.where(tm % 2 == 0, jnp.concatenate([att, partner]), jnp.concatenate([partner, att]))
    left = lax.ppermute(chip[2 * lat_dev :], "tm", up2)
    right = lax.ppermute(chip[: 6 * lat_dev], "tm", down2)
    features, msg = conv_stack(
        tm.reshape(1), (left, partner, right), att, stats,
        (cot_left, cot, cot_right), w_out, conv_weight, conv_bias,
    )

    msg = msg.reshape(pat_dev, lat_dev, width + 128)
    msgs = [msg] + [lax.ppermute(msg, "y", shift(NY, s)) for s in range(1, NY)]
    dq = backward_attention(y.reshape(1), kv, valid, queries, msgs)

    pieces = lax.all_to_all(dq, ("y", "tm"), 0, 0, tiled=True)
    dq_row = jnp.sum(pieces, axis=0, keepdims=True).astype(bf16)
    copies = jnp.broadcast_to(dq_row.reshape(1, width // 128, 128), (lat_rows, width // 128, 128))
    dq_all = lax.all_to_all(copies, ("y", "z", "tm"), 0, 0, tiled=True)
    d_latents = nt_dot(dq_all.reshape(lat_rows, width), w_query)
    return features.reshape(pat_dev, lat_dev, width), d_latents


def solution(mesh):
    split = Mesh(mesh.devices.reshape(NY, NZ, NTM), ("y", "z", "tm"))
    contacts = ("y", "z")
    in_specs = (P(contacts, "tm"), P(contacts), P(contacts)) + (P(),) * 8 + (P("tm", contacts, None),)
    out_specs = (P("tm", contacts, None), P())
    return jax.shard_map(local, mesh=split, in_specs=in_specs, out_specs=out_specs, check_vma=False)
```

time: 169 us -> 187 us (1.11)
  Pallas kernels: 57.9 us -> 73.1 us
  local copies, waits for them, and re-layouts: 10.1 us -> 24.3 us
  starting transfers between devices: 43.3 us -> 34.9 us
  blocking collectives: 42.6 us -> 39.1 us
  waiting for transfers between devices: 6.6 us -> 9.97 us
  other arithmetic: 4.07 us -> 1.82 us
    unnamed x34 -> x24, local copies, waits for them, and re-layouts: 2.82 us -> 23.4 us
    pallas_call x2 -> x5, Pallas kernels: 37.7 us -> 54 us  [absorb(): pl.pallas_call(functools.partial(absorb_kernel, fresh=fresh, last=last, c...]
    ppermute x14 -> x16, starting transfers between devices: 35.3 us -> 28.5 us  [the longest x3 9.36 us: local(): above = lax.ppermute(above, 'z', shift(NZ, -1))]
    all_to_all x2, blocking collectives: 42.6 us -> 39.1 us  [the longest x1 24 us: local(): dq_all = lax.all_to_all(copies, ('y', 'z', 'tm'), 0, 0, tiled=True)]
    ppermute x14 -> x16, waiting for transfers between devices: 6.59 us -> 9.97 us  [the longest x1 3.52 us: local(): right = lax.ppermute(chip[:6 * lat_dev], 'tm', down2)]
    pallas_call x1, Pallas kernels: 13.1 us -> 15.9 us  [backward_attention(): pl.pallas_call(backward_kernel, grid=(windows,), in_specs=[pl.BlockSpec(m...]
    pallas_call x1, Pallas kernels: 5.11 us -> 2.8 us  [conv_stack(): pl.pallas_call(conv_kernel, in_specs=[pl.BlockSpec(memory_space=pltpu.SME...]
    broadcast_in_dim x1 -> x0, other arithmetic: 2.21 us -> none  [local(): jnp.broadcast_to(dq_row, (lat_rows, width))]
  transfers between devices with their start and end apart: 16 -> 18, of which waited for: 5 -> 6; matrix products, arithmetic and copies ran while one was open for 1% -> 1% of each run, Pallas kernels for 1% -> 26%
where the time goes in v2:
time: 187 us; the launch traced here: 186 us
  Pallas kernels  73.1 us (39%)
  blocking collectives  39.1 us (21%)
  starting transfers between devices  34.9 us (19%)
  local copies, waits for them, and re-layouts  24.3 us (13%)
  waiting for transfers between devices  9.97 us (5%)
    pallas_call x5, Pallas kernels, absorb(): pl.pallas_call(functools.partial(absorb_kernel, fresh=fresh, last=last, c...  54 us
    all_to_all x1, blocking collectives, local(): dq_all = lax.all_to_all(copies, ('y', 'z', 'tm'), 0, 0, tiled=True)  24 us
    unnamed x24, local copies, waits for them, and re-layouts  23.4 us
    pallas_call x1, Pallas kernels, backward_attention(): pl.pallas_call(backward_kernel, grid=(windows,), in_specs=[pl.BlockSpec(m...  15.9 us
    all_to_all x1, blocking collectives, local(): pieces = lax.all_to_all(dq, ('y', 'tm'), 0, 0, tiled=True)  15.1 us
    ppermute x3, starting transfers between devices, local(): above = lax.ppermute(above, 'z', shift(NZ, -1))  9.36 us
    ppermute x3, starting transfers between devices, local(): lax.ppermute(parts[s], 'y', shift(NY, -s))  5.61 us
    ppermute x1, starting transfers between devices, local(): left = lax.ppermute(chip[2 * lat_dev:], 'tm', up2)  5.38 us
  transfers between devices with their start and end apart: 18, of which 6 were waited for; matrix products, arithmetic and copies ran while one was open for 1% of the time, Pallas kernels for 26%

profile of v2, /device:TPU:1, one launch (start us, length us, event | category | flops | bytes accessed | tf_op | source)
XLA Modules:
  0.0 186.0 jit_solution(11578089662378921584)
XLA Ops:
  0.6 0.0 copy-start
  0.7 0.7 and_select_fusion.1
  2.1 0.1 select_convert_fusion
  2.2 0.9 pad_maximum_fusion.refs_0_
  3.1 2.5 %collective-permute-start = (bf16[256,256]{1,0:T(8,128)(2,1)S(1)}, bf16[256,256]{1,0:T(8,128)(2,1)S(1)}, u32[]{:S(2)}, u32[]{:S(2)}) collective-permute-start(bf16[256,256]{1,0:T(8,128)(2,1)S(1)} %pad_maximum_fusion.refs_0_), channel_id=1, source_target_pairs={{0,8},{8,16},{16,24},{24,32},{32,40},{40,48},{48,56},{56,0},{1,9},... | collective-permute-start | bytes 393224 | tf_op jit(solution)/shard_map/ppermute | solution.py:437
  5.6 4.0 %collective-permute-start.1 = (bf16[256,256]{1,0:T(8,128)(2,1)S(1)}, bf16[256,256]{1,0:T(8,128)(2,1)S(1)}, u32[]{:S(2)}, u32[]{:S(2)}) collective-permute-start(bf16[256,256]{1,0:T(8,128)(2,1)S(1)} %pad_maximum_fusion.refs_0_), channel_id=1, source_target_pairs={{0,56},{8,0},{16,8},{24,16},{32,24},{40,32},{48,40},{56,48},{1,57}... | collective-permute-start | bytes 393224 | tf_op jit(solution)/shard_map/ppermute | solution.py:439
  9.6 0.7 dynamic-slice_bitcast_fusion.3
  10.4 0.2 convolution_convert_fusion.refs_1_.refs_2_.q_ref
  10.6 2.2 %copy-done.4 = bf16[4096,512]{1,0:T(8,128)(2,1)S(1)} copy-done((bf16[4096,512]{1,0:T(8,128)(2,1)S(1)}, bf16[4096,512]{1,0:T(8,128)(2,1)}, u32[]{:S(2)}) %copy-start.4) | copy-done | bytes 4194328
  12.8 1.2 copy-done.6
  14.0 0.8 copy-done.8
  14.8 5.8 %absorb.5 = (bf16[4,2048,1024]{2,1,0:T(8,128)(2,1)S(1)}, f32[8,2048]{1,0:T(8,128)S(1)}, f32[4,256,512]{2,1,0:T(8,128)S(1)}, f32[4,256,128]{2,1,0:T(8,128)S(1)}) custom-call(bf16[256,256]{1,0:T(8,128)(2,1)S(1)} %pad_maximum_fusion.refs_0_, bf16[32,512]{1,0:T(8,128)(2,1)S(1)} %convolution_convert_fusion.refs_1_.refs_2_.q_ref, bf16[32,512]{1,0:T(8,128)(2,1)S(1)} %copy-done.8, ...), custom_call_target="tpu_custom_call" | custom-call | tf_op jit(solution)/shard_map/absorb/pallas_call | solution.py:196
  20.6 5.7 %copy-done.1 = bf16[4,2048,1024]{2,1,0:T(8,128)(2,1)} copy-done((bf16[4,2048,1024]{2,1,0:T(8,128)(2,1)}, bf16[4,2048,1024]{2,1,0:T(8,128)(2,1)S(1)}, u32[]{:S(2)}) %copy-start.1) | copy-done | bytes 16777240
  26.3 0.0 collective-permute-done.refs_0_
  26.4 0.0 collective-permute-done.1.refs_1_
  26.4 0.0 collective-permute-start.2
  26.4 2.7 %collective-permute-start.3 = (bf16[256,256]{1,0:T(8,128)(2,1)S(1)}, bf16[256,256]{1,0:T(8,128)(2,1)S(1)}, u32[]{:S(2)}, u32[]{:S(2)}) collective-permute-start(bf16[256,256]{1,0:T(8,128)(2,1)S(1)} %collective-permute-done.1.refs_1_), channel_id=1, source_target_pairs={{0,56},{8,0},{16,8},{24,16},{32,24},{40,32},{48,40},{56,48},{1,57}... | collective-permute-start | bytes 393224 | tf_op jit(solution)/shard_map/ppermute | solution.py:439
  29.0 4.5 %collective-permute-start.4 = (bf16[24,512]{1,0:T(8,128)(2,1)S(1)}, bf16[24,512]{1,0:T(8,128)(2,1)S(1)}, u32[]{:S(2)}, u32[]{:S(2)}) collective-permute-start(bf16[24,512]{1,0:T(8,128)(2,1)S(1)} %get-tuple-element.83), channel_id=1, source_target_pairs={{0,1},{1,2},{2,3},{3,4},{4,5},{5,6},{6,7},{8,9},{9,10},{10,11},{11... | collective-permute-start | bytes 73736 | tf_op jit(solution)/shard_map/ppermute | solution.py:431
  33.6 1.9 %collective-permute-start.5 = (bf16[24,512]{1,0:T(8,128)(2,1)S(1)}, bf16[24,512]{1,0:T(8,128)(2,1)S(1)}, u32[]{:S(2)}, u32[]{:S(2)}) collective-permute-start(bf16[24,512]{1,0:T(8,128)(2,1)S(1)} %get-tuple-element.82), channel_id=1, source_target_pairs={{1,0},{2,1},{3,2},{4,3},{5,4},{6,5},{7,6},{9,8},{10,9},{11,10},{12... | collective-permute-start | bytes 73736 | tf_op jit(solution)/shard_map/ppermute | solution.py:432
  35.5 0.0 copy-done.5
  35.5 13.9 %absorb.6 = (bf16[4,2048,1024]{2,1,0:T(8,128)(2,1)}, f32[8,2048]{1,0:T(8,128)S(1)}, f32[4,256,512]{2,1,0:T(8,128)S(1)}, f32[4,256,128]{2,1,0:T(8,128)S(1)}) custom-call(bf16[256,256]{1,0:T(8,128)(2,1)S(1)} %collective-permute-done.refs_0_, bf16[256,256]{1,0:T(8,128)(2,1)S(1)} %collective-permute-done.1.refs_1_, ...), custom_call_target="tpu_custom_call", output_to_operand_aliasing={{0}: (6, {}), {1}: (7, {})} | custom-call | tf_op jit(solution)/shard_map/absorb/pallas_call | solution.py:196
  49.4 0.0 collective-permute-done.4.cl_ref
  49.4 0.0 collective-permute-done.5.cr_ref
  49.4 0.0 collective-permute-done.2.refs_0_
  49.4 0.0 collective-permute-done.3.refs_1_
  49.4 0.1 collective-permute-start.6
  49.5 2.7 %collective-permute-start.7 = (bf16[256,256]{1,0:T(8,128)(2,1)S(1)}, bf16[256,256]{1,0:T(8,128)(2,1)S(1)}, u32[]{:S(2)}, u32[]{:S(2)}) collective-permute-start(bf16[256,256]{1,0:T(8,128)(2,1)S(1)} %collective-permute-done.3.refs_1_), channel_id=1, source_target_pairs={{0,56},{8,0},{16,8},{24,16},{32,24},{40,32},{48,40},{56,48},{1,57}... | collective-permute-start | bytes 393224 | tf_op jit(solution)/shard_map/ppermute | solution.py:439
  52.2 13.9 %absorb.7 = (bf16[4,2048,1024]{2,1,0:T(8,128)(2,1)}, f32[8,2048]{1,0:T(8,128)S(1)}, f32[4,256,512]{2,1,0:T(8,128)S(1)}, f32[4,256,128]{2,1,0:T(8,128)S(1)}) custom-call(bf16[256,256]{1,0:T(8,128)(2,1)S(1)} %collective-permute-done.2.refs_0_, bf16[256,256]{1,0:T(8,128)(2,1)S(1)} %collective-permute-done.3.refs_1_, ...), custom_call_target="tpu_custom_call", output_to_operand_aliasing={{0}: (6, {}), {1}: (7, {})} | custom-call | tf_op jit(solution)/shard_map/absorb/pallas_call | solution.py:196
  66.0 0.0 collective-permute-done.6.refs_0_
  66.0 0.0 collective-permute-done.7.refs_1_
  66.0 0.0 collective-permute-start.8
  66.1 14.0 %absorb.8 = (bf16[4,2048,1024]{2,1,0:T(8,128)(2,1)}, f32[8,2048]{1,0:T(8,128)S(1)}, f32[4,256,512]{2,1,0:T(8,128)S(1)}, f32[4,256,128]{2,1,0:T(8,128)S(1)}) custom-call(bf16[256,256]{1,0:T(8,128)(2,1)S(1)} %collective-permute-done.6.refs_0_, bf16[256,256]{1,0:T(8,128)(2,1)S(1)} %collective-permute-done.7.refs_1_, ...), custom_call_target="tpu_custom_call", output_to_operand_aliasing={{0}: (6, {}), {1}: (7, {})} | custom-call | tf_op jit(solution)/shard_map/absorb/pallas_call | solution.py:196
  80.0 0.0 collective-permute-done.8.refs_0_
  80.0 5.8 %copy-done.2 = bf16[4,2048,1024]{2,1,0:T(8,128)(2,1)S(1)} copy-done((bf16[4,2048,1024]{2,1,0:T(8,128)(2,1)S(1)}, bf16[4,2048,1024]{2,1,0:T(8,128)(2,1)}, u32[]{:S(2)}) %copy-start.2) | copy-done | bytes 16777240
  85.8 6.4 %absorb.9 = (bf16[4,2048,1024]{2,1,0:T(8,128)(2,1)S(1)}, f32[8,2048]{1,0:T(8,128)S(1)}, f32[4,8,640]{2,1,0:T(8,128)S(1)}, f32[4,8,640]{2,1,0:T(8,128)S(1)}, f32[...) custom-call(bf16[256,256]{1,0:T(8,128)(2,1)S(1)} %collective-permute-done.8.refs_0_, ...), custom_call_target="tpu_custom_call", output_to_operand_aliasing={{0}: (5, {}), {1}: (6, {})} | custom-call | tf_op jit(solution)/shard_map/absorb/pallas_call | solution.py:196
  92.3 5.7 %copy-done.3 = bf16[4,2048,1024]{2,1,0:T(8,128)(2,1)} copy-done((bf16[4,2048,1024]{2,1,0:T(8,128)(2,1)}, bf16[4,2048,1024]{2,1,0:T(8,128)(2,1)S(1)}, u32[]{:S(2)}) %copy-start.3) | copy-done | bytes 16777240
  98.0 2.9 %collective-permute-start.10 = (f32[4,8,640]{2,1,0:T(8,128)S(1)}, f32[4,8,640]{2,1,0:T(8,128)S(1)}, u32[]{:S(2)}, u32[]{:S(2)}) collective-permute-start(f32[4,8,640]{2,1,0:T(8,128)S(1)} %get-tuple-element.66), channel_id=1, source_target_pairs={{0,128},{64,192},{128,0},{192,64},{1,129},{65,193},{129,1},{193,65... | collective-permute-start | bytes 245768 | tf_op jit(solution)/shard_map/ppermute | solution.py:451
  100.9 0.4 collective-permute-start.11
  101.3 2.3 %collective-permute-start.9 = (f32[4,8,640]{2,1,0:T(8,128)S(1)}, f32[4,8,640]{2,1,0:T(8,128)S(1)}, u32[]{:S(2)}, u32[]{:S(2)}) collective-permute-start(f32[4,8,640]{2,1,0:T(8,128)S(1)} %get-tuple-element.65), channel_id=1, source_target_pairs={{0,192},{64,0},{128,64},{192,128},{1,193},{65,1},{129,65},{193,129... | collective-permute-start | bytes 245768 | tf_op jit(solution)/shard_map/ppermute | solution.py:451
  103.6 0.0 collective-permute-done.10.refs_2_
  103.6 1.8 collective-permute-done.11.refs_3_
  105.4 0.0 collective-permute-done.9.refs_1_
  105.4 0.4 combine_parts.1
  105.8 0.1 collective-permute-start.12
  106.0 1.2 collective-permute-done.12.partner_ref
  107.2 5.4 %collective-permute-start.13 = (bf16[48,512]{1,0:T(8,128)(2,1)S(1)}, bf16[48,512]{1,0:T(8,128)(2,1)S(1)}, u32[]{:S(2)}, u32[]{:S(2)}) collective-permute-start(bf16[48,512]{1,0:T(8,128)(2,1)S(1)} %get-tuple-element.81), channel_id=1, source_target_pairs={{0,2},{1,3},{2,4},{3,5},{4,6},{5,7},{8,10},{9,11},{10,12},{11,13},... | collective-permute-start | bytes 147464 | tf_op jit(solution)/shard_map/ppermute | solution.py:456
  112.6 1.3 collective-permute-start.14
  113.9 0.0 collective-permute-done.13.left_ref
  113.9 3.5 %collective-permute-done.14.right_ref = bf16[48,512]{1,0:T(8,128)(2,1)S(1)} collective-permute-done((bf16[48,512]{1,0:T(8,128)(2,1)S(1)}, bf16[48,512]{1,0:T(8,128)(2,1)S(1)}, u32[]{:S(2)}, u32[]{:S(2)}) %collective-permute-start.14) | collective-permute-done | bytes 49184 | tf_op jit(solution)/shard_map/ppermute | solution.py:457
  117.4 1.9 %copy-done.7 = bf16[2,3,512,512]{3,2,1,0:T(8,128)(2,1)S(1)} copy-done((bf16[2,3,512,512]{3,2,1,0:T(8,128)(2,1)S(1)}, bf16[2,3,512,512]{3,2,1,0:T(8,128)(2,1)}, u32[]{:S(2)}) %copy-start.7) | copy-done | bytes 3145752
  119.3 2.8 %conv_stack.1 = (bf16[32,512]{1,0:T(8,128)(2,1)}, bf16[32,640]{1,0:T(8,128)(2,1)S(1)}) custom-call(s32[1]{0:T(128)} %bitcast.tm_ref, bf16[48,512]{1,0:T(8,128)(2,1)S(1)} %collective-permute-done.13.left_ref, bf16[32,512]{1,0:T(8,128)(2,1)S(1)} %get-tuple-element.68.own_ref, bf16[32,512]{1,0:T(8,128)(2,1)S(1)} %collective-permute-done.12.partner_ref, ...), custom_call_target="tpu_custom_call" | custom-call | tf_op jit(solution)/shard_map/conv_stack/pallas_call | solution.py:315
  122.1 0.0 collective-permute-start.15
  122.1 4.1 %collective-permute-start.16 = (bf16[4,8,640]{2,1,0:T(8,128)(2,1)S(1)}, bf16[4,8,640]{2,1,0:T(8,128)(2,1)S(1)}, u32[]{:S(2)}, u32[]{:S(2)}) collective-permute-start(bf16[4,8,640]{2,1,0:T(8,128)(2,1)S(1)} %bitcast.36), channel_id=1, source_target_pairs={{0,128},{64,192},{128,0},{192,64},{1,129},{65,193},{129,1},{193,65... | collective-permute-start | bytes 122888 | tf_op jit(solution)/shard_map/ppermute | solution.py:464
  126.2 0.0 collective-permute-start.17
  126.2 0.2 collective-permute-done.15.refs_1_
  126.4 1.6 collective-permute-done.16.refs_2_
  128.1 1.6 collective-permute-done.17.refs_3_
  129.6 15.9 %backward_attention.1 = f32[32,512]{1,0:T(8,128)S(1)} custom-call(s32[1]{0:T(128)} %bitcast.12.y_ref, bf16[4,2048,1024]{2,1,0:T(8,128)(2,1)} %copy-done.3, f32[8,2048]{1,0:T(8,128)S(1)} %get-tuple-element.74.valid_ref, bf16[32,512]{1,0:T(8,128)(2,1)S(1)} %convolution_convert_fusion.refs_1_.refs_2_.q_ref, bf16[4,8,640]{2,1,0:T(8,128)(2,1)S(1)} %bitcast.38, ...), custom_call_target="tpu_custom_call" | custom-call | tf_op jit(solution)/shard_map/backward_attention/pallas_call | solution.py:379
  145.6 0.1 copy.22
  145.7 15.1 %all_to_all.14 = f32[32,1,512]{2,1,0:T(1,128)S(1)} all-to-all(f32[32,1,512]{2,1,0:T(1,128)S(1)} %copy.22), channel_id=1, replica_groups=mesh['y'=4,'z'=8,'tm'=8] {'y','tm'}, dimensions={0} | all-to-all | bytes 131072 | tf_op jit(solution)/shard_map/all_to_all | solution.py:467
  160.8 0.1 reduce_sum.9
  160.9 0.1 broadcast_in_dim.30
  160.9 24.0 %all_to_all.15 = bf16[256,4,128]{2,1,0:T(4,128)(2,1)S(1)} all-to-all(bf16[256,4,128]{2,1,0:T(4,128)(2,1)S(1)} %broadcast_in_dim.30), channel_id=1, replica_groups=mesh['y'=4,'z'=8,'tm'=8] {'y','z','tm'}, dimensions={0} | all-to-all | bytes 524288 | tf_op jit(solution)/shard_map/all_to_all | solution.py:470
  184.9 1.1 fusion
  (19 shorter events, 0.1 us)
Async XLA Ops:
  0.6 9.7 %copy-start = (bf16[512,512]{1,0:T(8,128)(2,1)S(1)}, bf16[512,512]{1,0:T(8,128)(2,1)}, u32[]{:S(2)}) copy-start(bf16[512,512]{1,0:T(8,128)(2,1)} %param.19) | copy-start | bytes 1572868
  0.6 28.4 %copy-start.10 = (bf16[4,8,512]{2,1,0:T(8,128)(2,1)S(1)}, bf16[4,8,512]{2,1,0:T(8,128)(2,1)}, u32[]{:S(2)}) copy-start(bf16[4,8,512]{2,1,0:T(8,128)(2,1)} %param.23) | copy-start | bytes 98308
  3.1 23.3 %collective-permute-start = (bf16[256,256]{1,0:T(8,128)(2,1)S(1)}, bf16[256,256]{1,0:T(8,128)(2,1)S(1)}, u32[]{:S(2)}, u32[]{:S(2)}) collective-permute-start(bf16[256,256]{1,0:T(8,128)(2,1)S(1)} %pad_maximum_fusion.refs_0_), channel_id=1, source_target_pairs={{0,8},{8,16},{16,24},{24,32},{32,40},{40,48},{48,56},{56,0},{1,9},... | collective-permute-start | bytes 393224 | tf_op jit(solution)/shard_map/ppermute | solution.py:437
  5.6 20.8 %collective-permute-start.1 = (bf16[256,256]{1,0:T(8,128)(2,1)S(1)}, bf16[256,256]{1,0:T(8,128)(2,1)S(1)}, u32[]{:S(2)}, u32[]{:S(2)}) collective-permute-start(bf16[256,256]{1,0:T(8,128)(2,1)S(1)} %pad_maximum_fusion.refs_0_), channel_id=1, source_target_pairs={{0,56},{8,0},{16,8},{24,16},{32,24},{40,32},{48,40},{56,48},{1,57}... | collective-permute-start | bytes 393224 | tf_op jit(solution)/shard_map/ppermute | solution.py:439
  10.6 2.2 %copy-start.4 = (bf16[4096,512]{1,0:T(8,128)(2,1)S(1)}, bf16[4096,512]{1,0:T(8,128)(2,1)}, u32[]{:S(2)}) copy-start(bf16[4096,512]{1,0:T(8,128)(2,1)} %refs_4_.9) | copy-start | bytes 12582916
  12.8 1.2 copy-start.6
  14.0 0.8 copy-start.8
  14.7 20.8 %copy-start.5 = (bf16[4096,512]{1,0:T(8,128)(2,1)S(1)}, bf16[4096,512]{1,0:T(8,128)(2,1)}, u32[]{:S(2)}) copy-start(bf16[4096,512]{1,0:T(8,128)(2,1)} %refs_4_.9) | copy-start | bytes 12582916
  20.6 5.7 %copy-start.1 = (bf16[4,2048,1024]{2,1,0:T(8,128)(2,1)}, bf16[4,2048,1024]{2,1,0:T(8,128)(2,1)S(1)}, u32[]{:S(2)}) copy-start(bf16[4,2048,1024]{2,1,0:T(8,128)(2,1)S(1)} %get-tuple-element.42.refs_6_) | copy-start | bytes 50331652
  26.4 23.1 %collective-permute-start.2 = (bf16[256,256]{1,0:T(8,128)(2,1)S(1)}, bf16[256,256]{1,0:T(8,128)(2,1)S(1)}, u32[]{:S(2)}, u32[]{:S(2)}) collective-permute-start(bf16[256,256]{1,0:T(8,128)(2,1)S(1)} %collective-permute-done.refs_0_), channel_id=1, source_target_pairs={{0,8},{8,16},{16,24},{24,32},{32,40},{40,48},{48,56},{56,0},{1,9},... | collective-permute-start | bytes 393224 | tf_op jit(solution)/shard_map/ppermute | solution.py:437
  26.4 23.1 %collective-permute-start.3 = (bf16[256,256]{1,0:T(8,128)(2,1)S(1)}, bf16[256,256]{1,0:T(8,128)(2,1)S(1)}, u32[]{:S(2)}, u32[]{:S(2)}) collective-permute-start(bf16[256,256]{1,0:T(8,128)(2,1)S(1)} %collective-permute-done.1.refs_1_), channel_id=1, source_target_pairs={{0,56},{8,0},{16,8},{24,16},{32,24},{40,32},{48,40},{56,48},{1,57}... | collective-permute-start | bytes 393224 | tf_op jit(solution)/shard_map/ppermute | solution.py:439
  29.0 20.4 %collective-permute-start.4 = (bf16[24,512]{1,0:T(8,128)(2,1)S(1)}, bf16[24,512]{1,0:T(8,128)(2,1)S(1)}, u32[]{:S(2)}, u32[]{:S(2)}) collective-permute-start(bf16[24,512]{1,0:T(8,128)(2,1)S(1)} %get-tuple-element.83), channel_id=1, source_target_pairs={{0,1},{1,2},{2,3},{3,4},{4,5},{5,6},{6,7},{8,9},{9,10},{10,11},{11... | collective-permute-start | bytes 73736 | tf_op jit(solution)/shard_map/ppermute | solution.py:431
  33.6 15.8 %collective-permute-start.5 = (bf16[24,512]{1,0:T(8,128)(2,1)S(1)}, bf16[24,512]{1,0:T(8,128)(2,1)S(1)}, u32[]{:S(2)}, u32[]{:S(2)}) collective-permute-start(bf16[24,512]{1,0:T(8,128)(2,1)S(1)} %get-tuple-element.82), channel_id=1, source_target_pairs={{1,0},{2,1},{3,2},{4,3},{5,4},{6,5},{7,6},{9,8},{10,9},{11,10},{12... | collective-permute-start | bytes 73736 | tf_op jit(solution)/shard_map/ppermute | solution.py:432
  49.4 16.6 %collective-permute-start.6 = (bf16[256,256]{1,0:T(8,128)(2,1)S(1)}, bf16[256,256]{1,0:T(8,128)(2,1)S(1)}, u32[]{:S(2)}, u32[]{:S(2)}) collective-permute-start(bf16[256,256]{1,0:T(8,128)(2,1)S(1)} %collective-permute-done.2.refs_0_), channel_id=1, source_target_pairs={{0,8},{8,16},{16,24},{24,32},{32,40},{40,48},{48,56},{56,0},{1,9},... | collective-permute-start | bytes 393224 | tf_op jit(solution)/shard_map/ppermute | solution.py:437
  49.5 16.5 %collective-permute-start.7 = (bf16[256,256]{1,0:T(8,128)(2,1)S(1)}, bf16[256,256]{1,0:T(8,128)(2,1)S(1)}, u32[]{:S(2)}, u32[]{:S(2)}) collective-permute-start(bf16[256,256]{1,0:T(8,128)(2,1)S(1)} %collective-permute-done.3.refs_1_), channel_id=1, source_target_pairs={{0,56},{8,0},{16,8},{24,16},{32,24},{40,32},{48,40},{56,48},{1,57}... | collective-permute-start | bytes 393224 | tf_op jit(solution)/shard_map/ppermute | solution.py:439
  66.0 14.0 %collective-permute-start.8 = (bf16[256,256]{1,0:T(8,128)(2,1)S(1)}, bf16[256,256]{1,0:T(8,128)(2,1)S(1)}, u32[]{:S(2)}, u32[]{:S(2)}) collective-permute-start(bf16[256,256]{1,0:T(8,128)(2,1)S(1)} %collective-permute-done.6.refs_0_), channel_id=1, source_target_pairs={{0,8},{8,16},{16,24},{24,32},{32,40},{40,48},{48,56},{56,0},{1,9},... | collective-permute-start | bytes 393224 | tf_op jit(solution)/shard_map/ppermute | solution.py:437
  80.0 5.8 %copy-start.2 = (bf16[4,2048,1024]{2,1,0:T(8,128)(2,1)S(1)}, bf16[4,2048,1024]{2,1,0:T(8,128)(2,1)}, u32[]{:S(2)}) copy-start(bf16[4,2048,1024]{2,1,0:T(8,128)(2,1)} %get-tuple-element.60.refs_5_) | copy-start | bytes 50331652
  85.8 31.6 %copy-start.9 = (bf16[512,512]{1,0:T(8,128)(2,1)S(1)}, bf16[512,512]{1,0:T(8,128)(2,1)}, u32[]{:S(2)}) copy-start(bf16[512,512]{1,0:T(8,128)(2,1)} %w_out_ref.1) | copy-start | bytes 1572868
  85.8 31.6 %copy-start.11 = (f32[2,512]{1,0:T(2,128)S(1)}, f32[2,512]{1,0:T(2,128)}, u32[]{:S(2)}) copy-start(f32[2,512]{1,0:T(2,128)} %bias_ref.1) | copy-start | bytes 12292
  92.2 5.7 %copy-start.3 = (bf16[4,2048,1024]{2,1,0:T(8,128)(2,1)}, bf16[4,2048,1024]{2,1,0:T(8,128)(2,1)S(1)}, u32[]{:S(2)}) copy-start(bf16[4,2048,1024]{2,1,0:T(8,128)(2,1)S(1)} %get-tuple-element.73.kv_ref) | copy-start | bytes 50331652
  98.0 5.6 %collective-permute-start.10 = (f32[4,8,640]{2,1,0:T(8,128)S(1)}, f32[4,8,640]{2,1,0:T(8,128)S(1)}, u32[]{:S(2)}, u32[]{:S(2)}) collective-permute-start(f32[4,8,640]{2,1,0:T(8,128)S(1)} %get-tuple-element.66), channel_id=1, source_target_pairs={{0,128},{64,192},{128,0},{192,64},{1,129},{65,193},{129,1},{193,65... | collective-permute-start | bytes 245768 | tf_op jit(solution)/shard_map/ppermute | solution.py:451
  100.9 4.5 %collective-permute-start.11 = (f32[4,8,640]{2,1,0:T(8,128)S(1)}, f32[4,8,640]{2,1,0:T(8,128)S(1)}, u32[]{:S(2)}, u32[]{:S(2)}) collective-permute-start(f32[4,8,640]{2,1,0:T(8,128)S(1)} %get-tuple-element.67), channel_id=1, source_target_pairs={{0,64},{64,128},{128,192},{192,0},{1,65},{65,129},{129,193},{193,1... | collective-permute-start | bytes 245768 | tf_op jit(solution)/shard_map/ppermute | solution.py:451
  101.3 4.1 %collective-permute-start.9 = (f32[4,8,640]{2,1,0:T(8,128)S(1)}, f32[4,8,640]{2,1,0:T(8,128)S(1)}, u32[]{:S(2)}, u32[]{:S(2)}) collective-permute-start(f32[4,8,640]{2,1,0:T(8,128)S(1)} %get-tuple-element.65), channel_id=1, source_target_pairs={{0,192},{64,0},{128,64},{192,128},{1,193},{65,1},{129,65},{193,129... | collective-permute-start | bytes 245768 | tf_op jit(solution)/shard_map/ppermute | solution.py:451
  105.8 1.3 collective-permute-start.12
  107.2 6.7 %collective-permute-start.13 = (bf16[48,512]{1,0:T(8,128)(2,1)S(1)}, bf16[48,512]{1,0:T(8,128)(2,1)S(1)}, u32[]{:S(2)}, u32[]{:S(2)}) collective-permute-start(bf16[48,512]{1,0:T(8,128)(2,1)S(1)} %get-tuple-element.81), channel_id=1, source_target_pairs={{0,2},{1,3},{2,4},{3,5},{4,6},{5,7},{8,10},{9,11},{10,12},{11,13},... | collective-permute-start | bytes 147464 | tf_op jit(solution)/shard_map/ppermute | solution.py:456
  112.6 4.8 %collective-permute-start.14 = (bf16[48,512]{1,0:T(8,128)(2,1)S(1)}, bf16[48,512]{1,0:T(8,128)(2,1)S(1)}, u32[]{:S(2)}, u32[]{:S(2)}) collective-permute-start(bf16[48,512]{1,0:T(8,128)(2,1)S(1)} %get-tuple-element.80), channel_id=1, source_target_pairs={{2,0},{3,1},{4,2},{5,3},{6,4},{7,5},{10,8},{11,9},{12,10},{13,11},... | collective-permute-start | bytes 147464 | tf_op jit(solution)/shard_map/ppermute | solution.py:457
  117.4 1.9 %copy-start.7 = (bf16[2,3,512,512]{3,2,1,0:T(8,128)(2,1)S(1)}, bf16[2,3,512,512]{3,2,1,0:T(8,128)(2,1)}, u32[]{:S(2)}) copy-start(bf16[2,3,512,512]{3,2,1,0:T(8,128)(2,1)} %conv_ref.1) | copy-start | bytes 9437188
  122.1 4.3 %collective-permute-start.15 = (bf16[4,8,640]{2,1,0:T(8,128)(2,1)S(1)}, bf16[4,8,640]{2,1,0:T(8,128)(2,1)S(1)}, u32[]{:S(2)}, u32[]{:S(2)}) collective-permute-start(bf16[4,8,640]{2,1,0:T(8,128)(2,1)S(1)} %bitcast.35), channel_id=1, source_target_pairs={{0,64},{64,128},{128,192},{192,0},{1,65},{65,129},{129,193},{193,1... | collective-permute-start | bytes 122888 | tf_op jit(solution)/shard_map/ppermute | solution.py:464
  122.1 6.0 %collective-permute-start.16 = (bf16[4,8,640]{2,1,0:T(8,128)(2,1)S(1)}, bf16[4,8,640]{2,1,0:T(8,128)(2,1)S(1)}, u32[]{:S(2)}, u32[]{:S(2)}) collective-permute-start(bf16[4,8,640]{2,1,0:T(8,128)(2,1)S(1)} %bitcast.36), channel_id=1, source_target_pairs={{0,128},{64,192},{128,0},{192,64},{1,129},{65,193},{129,1},{193,65... | collective-permute-start | bytes 122888 | tf_op jit(solution)/shard_map/ppermute | solution.py:464
  126.2 3.4 %collective-permute-start.17 = (bf16[4,8,640]{2,1,0:T(8,128)(2,1)S(1)}, bf16[4,8,640]{2,1,0:T(8,128)(2,1)S(1)}, u32[]{:S(2)}, u32[]{:S(2)}) collective-permute-start(bf16[4,8,640]{2,1,0:T(8,128)(2,1)S(1)} %bitcast.37), channel_id=1, source_target_pairs={{0,192},{64,0},{128,64},{192,128},{1,193},{65,1},{129,65},{193,129... | collective-permute-start | bytes 122888 | tf_op jit(solution)/shard_map/ppermute | solution.py:464

commit v3 on v2

--- a/solution.py
+++ b/solution.py
@@ -21,6 +21,8 @@
 
 NY, NZ, NTM = 4, 8, 8
 MIB = 1 << 20
+PIECE, PARTS, HALVES, VMEM_ABSORB = 2048, 2, 2, 28
+WUNROLL, VMEM_BACK = 4, 40
 
 
 def nt_dot(a, b):
@@ -85,65 +87,74 @@
     messages = [refs.pop(0) for _ in range(count)]
     q_ref, w_in_ref, w_kv_ref, table_ref = (refs.pop(0) for _ in range(4))
     if not fresh:
-        refs.pop(0), refs.pop(0)
         acc_in, stat_in = refs.pop(0), refs.pop(0)
-    kv_ref, valid_ref = refs.pop(0), refs.pop(0)
+    kv_hbm, valid_ref = refs.pop(0), refs.pop(0)
     if last:
         part_refs = [refs.pop(0) for _ in range(NY)]
     else:
         acc_out, stat_out = refs.pop(0), refs.pop(0)
-    pos_ref = refs.pop(0)
+    pos_ref, tok_ref, kv_ref, sem = refs
     width = q_ref.shape[1]
     heads = width // HD
     con_dev, span = messages[0].shape[0], messages[0].shape[1] - 128
-    step_no = pl.program_id(0)
-    message = messages[0][...]
-    if count == 2:
-        message = jnp.where(step_no == 0, message, messages[1][...])
+    windows = span // PATCH
+    rows = count * con_dev
+    message = jnp.concatenate([m[...] for m in messages], axis=0)
     sig = message[:, :span]
     meta = message[:, span:].astype(f32)
     idx = meta[:, 0:1] * 64.0 + meta[:, 1:2]
-    live = meta[0:1, 2:3]
     lane = lax.broadcasted_iota(jnp.int32, (1, con_dev), 1).astype(f32)
-    valid = jnp.where(lane < live, 1.0, 0.0)
+    valid = jnp.concatenate(
+        [jnp.where(lane < meta[c * con_dev : c * con_dev + 1, 2:3], 1.0, 0.0) for c in range(count)], axis=1
+    )
     valid_ref[...] = jnp.broadcast_to(valid, valid_ref.shape)
-    piece = 512
-    ids = lax.broadcasted_iota(jnp.int32, (con_dev, piece), 1).astype(f32)
-
-    def add_rows(k, pos):
-        for part in range(2):
-            start = pl.multiple_of((2 * k + part) * piece, piece)
-            hot = jnp.where(ids == idx - start.astype(f32), 1.0, 0.0).astype(bf16)
-            pos = pos + nn_dot(hot, table_ref[pl.ds(start, piece), :])
-        return pos
-
-    pos = lax.fori_loop(0, table_ref.shape[0] // (2 * piece), add_rows, jnp.zeros((con_dev, width), f32))
-    pos_ref[...] = pos
-    windows = span // PATCH
+    piece = PIECE
+    ids = lax.broadcasted_iota(jnp.int32, (rows, piece), 1).astype(f32)
+    pos_ref[...] = jnp.zeros_like(pos_ref)
+
+    @pl.loop(0, table_ref.shape[0] // piece)
+    def _(k):
+        start = pl.multiple_of(k * piece, piece)
+        hot = jnp.where(ids == idx - start.astype(f32), 1.0, 0.0).astype(bf16)
+        pos_ref[...] = pos_ref[...] + nn_dot(hot, table_ref[pl.ds(start, piece), :])
+
+    tall = jnp.concatenate([w_in_ref[...]] * windows, axis=0)
+    band = lax.broadcasted_iota(jnp.int32, sig.shape, 1) // PATCH
+    for w in range(windows):
+        embedded = nn_dot(jnp.where(band == w, sig, jnp.zeros_like(sig)), tall)
+        tok_ref[w * rows : (w + 1) * rows, :] = (embedded + pos_ref[...]).astype(bf16)
+    copies = []
+    for part in range(PARTS):
+        ws = windows // PARTS
+        tokens = tok_ref[part * ws * rows : (part + 1) * ws * rows, :]
+        for half in range(HALVES):
+            cols = slice(half * 2 * width // HALVES, (half + 1) * 2 * width // HALVES)
+            keyval = nn_dot(tokens, w_kv_ref[:, cols]).astype(bf16)
+            kv_ref[part * ws : (part + 1) * ws, :, cols] = keyval.reshape(ws, rows, 2 * width // HALVES)
+        copies.append(
+            pltpu.make_async_copy(
+                kv_ref.at[pl.ds(part * ws, ws)],
+                kv_hbm.at[pl.ds(part * ws, ws)],
+                sem.at[part],
+            )
+        )
+        copies[-1].start()
+    q_wide = spread_heads(q_ref[...], heads)
 
     def one_window(w):
-        pos = pos_ref[...]
-        q_wide = spread_heads(q_ref[...], heads)
-        tall = jnp.concatenate([w_in_ref[...]] * windows, axis=0)
-        band = lax.broadcasted_iota(jnp.int32, tall.shape, 0) // PATCH
-        embedded = nn_dot(sig, jnp.where(band == w, tall, jnp.zeros_like(tall)))
-        tokens = (embedded + pos).astype(bf16)
-        keyval = nn_dot(tokens, w_kv_ref[...]).astype(bf16)
-        kv_ref[w] = keyval
-        scores = nt_dot(q_wide, keyval[:, :width]) * scale_dot
+        scores = nt_dot(q_wide, kv_ref[w, :, :width]) * scale_dot
         scores = jnp.where(valid > 0.0, scores, neg_big)
         top = jnp.max(scores, axis=1, keepdims=True)
         if not fresh:
-            acc_now, stat_now = (acc_out, stat_out) if count > 1 else (acc_in, stat_in)
-            before, total_before, acc_before = stat_now[w, :, 0:1], stat_now[w, :, 1:2], acc_now[w]
+            before, total_before = stat_in[w, :, 0:1], stat_in[w, :, 1:2]
             top = jnp.maximum(top, before)
         weights = jnp.exp(scores - top)
         totals = jnp.sum(weights, axis=1, keepdims=True)
-        accum = nn_dot(weights.astype(bf16), keyval[:, width:])
+        accum = nn_dot(weights.astype(bf16), kv_ref[w, :, width:])
         if not fresh:
             fade = jnp.exp(before - top)
             totals = totals + total_before * fade
-            accum = accum + acc_before * fade
+            accum = accum + acc_in[w] * fade
         if not last:
             acc_out[w] = accum
             stat_out[w, :, 0:1] = top
@@ -158,58 +169,55 @@
                 part_ref[w, :, :width] = mixed[s * each : (s + 1) * each]
                 part_ref[w, :, width:] = stats[s * each : (s + 1) * each]
 
-    if count > 1:
-
-        @pl.when(step_no == 0)
-        def _():
-            acc_out[...] = acc_in[...]
-            stat_out[...] = stat_in[...]
-
-    @pl.loop(0, windows // 2)
+    together = WUNROLL // count
+
+    @pl.loop(0, windows // together)
     def _(k):
-        one_window(2 * k)
-        one_window(2 * k + 1)
-
-
-def absorb(messages, base, q, w_in, w_kv, table, state, last):
+        for part in range(together):
+            one_window(k * together + part)
+
+    for copy in copies:
+        copy.wait()
+
+
+def absorb(messages, q, w_in, w_kv, table, state, last):
     count = len(messages)
     lat, width = q.shape
     con_dev = messages[0].shape[0]
     windows = (messages[0].shape[1] - 128) // PATCH
     rows = lat * (width // HD)
     fresh = state is None
-    whole = lambda a: pl.BlockSpec(a.shape, lambda i: (0,) * a.ndim, pipeline_mode=pl.Buffered(1))
-    fixed = lambda shape: pl.BlockSpec(shape, lambda i: (0,) * len(shape), pipeline_mode=pl.Buffered(1))
-    anywhere = pl.BlockSpec(memory_space=pl.ANY)
+    vmem = pl.BlockSpec(memory_space=pltpu.VMEM)
+    hbm = pl.BlockSpec(memory_space=pltpu.HBM)
     operands = list(messages) + [q, w_in, w_kv, table]
-    in_specs = [whole(a) for a in operands]
+    in_specs = [vmem] * len(operands)
     aliases = {}
     if not fresh:
         n = len(operands)
         operands += list(state)
-        in_specs += [anywhere, anywhere] + [whole(a) for a in state[2:]]
-        aliases = {n: 0, n + 1: 1}
+        in_specs += [vmem, vmem]
+        aliases = {} if last else {n: 2, n + 1: 3}
     acc = jax.ShapeDtypeStruct((windows, rows, width), f32)
     stat = jax.ShapeDtypeStruct((windows, rows, 128), f32)
     part = jax.ShapeDtypeStruct((windows, lat // NY, width + 128), f32)
     tail = [part] * NY if last else [acc, stat]
     return pl.pallas_call(
         functools.partial(absorb_kernel, fresh=fresh, last=last, count=count),
-        grid=(count,),
         in_specs=in_specs,
-        out_specs=[
-            pl.BlockSpec((windows, con_dev, 2 * width), lambda i: (0, base + i, 0)),
-            pl.BlockSpec((8, con_dev), lambda i: (0, base + i)),
-        ]
-        + [fixed(a.shape) for a in tail],
+        out_specs=[hbm, vmem] + [vmem] * len(tail),
         out_shape=[
-            jax.ShapeDtypeStruct((windows, NZ * con_dev, 2 * width), bf16),
-            jax.ShapeDtypeStruct((8, NZ * con_dev), f32),
+            pltpu.HBM((windows, count * con_dev, 2 * width), bf16),
+            jax.ShapeDtypeStruct((8, count * con_dev), f32),
         ]
         + tail,
-        scratch_shapes=[pltpu.VMEM((con_dev, width), f32)],
+        scratch_shapes=[
+            pltpu.VMEM((count * con_dev, width), f32),
+            pltpu.VMEM((windows * count * con_dev, width), bf16),
+            pltpu.VMEM((windows, count * con_dev, 2 * width), bf16),
+            pltpu.SemaphoreType.DMA((PARTS,)),
+        ],
         input_output_aliases=aliases,
-        compiler_params=pltpu.CompilerParams(vmem_limit_bytes=28 * MIB),
+        compiler_params=pltpu.CompilerParams(vmem_limit_bytes=VMEM_ABSORB * MIB),
         name="absorb",
     )(*operands)
 
@@ -250,8 +258,11 @@
 
 def conv_kernel(
     tm_ref, left_ref, own_ref, partner_ref, right_ref, stats_ref, cl_ref, cot_ref, cr_ref,
-    w_out_ref, conv_ref, bias_ref, feat_ref, msg_ref, ext_ref,
+    w_out_ref, conv_hbm, bias_ref, feat_ref, msg_ref, ext_ref, conv_ref, sem,
 ):
+    weights = [pltpu.make_async_copy(conv_hbm.at[l], conv_ref.at[l], sem.at[l]) for l in range(LAYERS)]
+    for copy in weights:
+        copy.start()
     rows, width = own_ref.shape
     heads = width // HD
     windows = 4
@@ -274,10 +285,12 @@
     w_out = w_out_ref[...]
     x0 = rounded(nn_dot(att.astype(bf16), w_out))
     n0 = 14 * each
+    weights[0].wait()
     pre0 = bias_ref[0:1, :] + sum(nn_dot(x0[j * each : j * each + n0].astype(bf16), conv_ref[0, j]) for j in range(KSIZE))
     x1 = rounded(x0[each : each + n0] + jax.nn.silu(pre0))
     x1 = jnp.where(inside(1, 14), x1, 0.0)
     n1 = 10 * each
+    weights[1].wait()
     pre1 = bias_ref[1:2, :] + sum(nn_dot(x1[2 * j * each : 2 * j * each + n1].astype(bf16), conv_ref[1, j]) for j in range(KSIZE))
     feat_ref[...] = (x1[5 * each : 9 * each] + jax.nn.silu(pre1[3 * each : 7 * each])).astype(bf16)
     g2 = jnp.concatenate([r[...].astype(f32) for r in (cl_ref, cot_ref, cr_ref)], axis=0)
@@ -314,24 +327,28 @@
     vmem = pl.BlockSpec(memory_space=pltpu.VMEM)
     return pl.pallas_call(
         conv_kernel,
-        in_specs=[pl.BlockSpec(memory_space=pltpu.SMEM)] + [vmem] * 11,
+        in_specs=[pl.BlockSpec(memory_space=pltpu.SMEM)] + [vmem] * 9 + [pl.BlockSpec(memory_space=pltpu.HBM), vmem],
         out_specs=[vmem, vmem],
         out_shape=[
             jax.ShapeDtypeStruct((rows, width), bf16),
             jax.ShapeDtypeStruct((rows, width + 128), bf16),
         ],
-        scratch_shapes=[pltpu.VMEM((left.shape[0] + 2 * rows + right.shape[0], width), f32)],
+        scratch_shapes=[
+            pltpu.VMEM((left.shape[0] + 2 * rows + right.shape[0], width), f32),
+            pltpu.VMEM(conv_weight.shape, conv_weight.dtype),
+            pltpu.SemaphoreType.DMA((LAYERS,)),
+        ],
         compiler_params=pltpu.CompilerParams(vmem_limit_bytes=24 * MIB),
         name="conv_stack",
-    )(tm, left, own, partner, right, stats, cl, cot, cr, w_out, conv_weight, conv_bias)
-
-
-def backward_kernel(y_ref, kv_ref, valid_ref, q_ref, *refs):
-    *msg_refs, dq_ref, acc_ref = refs
+    )(tm, left, own, partner, right, stats, cl, cot, cr, w_out, pltpu.with_memory_space_constraint(conv_weight, pltpu.HBM), conv_bias)
+
+
+def backward_kernel(y_ref, q_ref, *refs, slots):
+    *refs, dq_ref, acc_ref = refs
+    msg_refs, refs = refs[:slots], refs[slots:]
+    kv_refs, valid_refs = refs[: len(refs) // 2], refs[len(refs) // 2 :]
     width = q_ref.shape[1]
     heads = width // HD
-    contacts = kv_ref.shape[1]
-    step = 256
     window = pl.program_id(0)
     msg = jnp.concatenate([r[0].astype(f32) for r in msg_refs], axis=0)
     terms = msg[:, width:]
@@ -346,52 +363,45 @@
     def _():
         acc_ref[...] = jnp.zeros_like(acc_ref)
 
-    def one_chunk(start):
-        rows = pl.ds(pl.multiple_of(start, step), step)
-        key_rows = kv_ref[0, rows, :width]
+    accum = acc_ref[...]
+    for kv_ref, valid_ref in zip(kv_refs, valid_refs):
+        key_rows = kv_ref[0, :, :width]
         scores = nt_dot(q_wide, key_rows) * scale_dot
-        scores = jnp.where(valid_ref[0:1, rows] > 0.0, scores, neg_big)
+        scores = jnp.where(valid_ref[0:1, :] > 0.0, scores, neg_big)
         prob = jnp.exp(scores - top) * inverse
-        grad_prob = nt_dot(grad_wide, kv_ref[0, rows, width:])
+        grad_prob = nt_dot(grad_wide, kv_ref[0, :, width:])
         dscore = (prob * (grad_prob - delta)).astype(bf16)
-        acc_ref[...] = acc_ref[...] + nn_dot(dscore, key_rows)
-
-    @pl.loop(0, contacts // step // 2)
-    def _(k):
-        one_chunk(2 * k * step)
-        one_chunk((2 * k + 1) * step)
+        accum = accum + nn_dot(dscore, key_rows)
+    acc_ref[...] = accum
 
     @pl.when(window == pl.num_programs(0) - 1)
     def _():
         dq = collect_heads(acc_ref[...], heads) * scale_dot
-        slots = len(msg_refs)
         each = dq.shape[0] // slots
         for s in range(slots):
             place = pl.multiple_of(((y_ref[0] + (slots - s)) % slots) * each, each)
             dq_ref[pl.ds(place, each), :] = dq[s * each : (s + 1) * each]
 
 
-def backward_attention(y, kv, valid, q, msgs):
-    windows, contacts, wide = kv.shape
+def backward_attention(y, kvs, valids, q, msgs):
+    windows = kvs[0].shape[0]
     lat, width = q.shape
     heads = width // HD
     whole = lambda a: pl.BlockSpec(a.shape, lambda p: (0,) * a.ndim, pipeline_mode=pl.Buffered(1))
+    kvs = [pltpu.with_memory_space_constraint(kv, pltpu.HBM) for kv in kvs]
+    each_window = lambda a: pl.BlockSpec((1,) + a.shape[1:], lambda p: (p, 0, 0))
     return pl.pallas_call(
-        backward_kernel,
+        functools.partial(backward_kernel, slots=len(msgs)),
         grid=(windows,),
-        in_specs=[
-            pl.BlockSpec(memory_space=pltpu.SMEM),
-            pl.BlockSpec((1, contacts, wide), lambda p: (p, 0, 0)),
-            whole(valid),
-            whole(q),
-        ]
-        + [pl.BlockSpec((1,) + m.shape[1:], lambda p: (p, 0, 0)) for m in msgs],
+        in_specs=[pl.BlockSpec(memory_space=pltpu.SMEM), whole(q)]
+        + [each_window(a) for a in (*msgs, *kvs)]
+        + [whole(v) for v in valids],
         out_specs=pl.BlockSpec((lat, width), lambda p: (0, 0)),
         out_shape=jax.ShapeDtypeStruct((lat, width), f32),
         scratch_shapes=[pltpu.VMEM((lat * heads, width), f32)],
-        compiler_params=pltpu.CompilerParams(vmem_limit_bytes=52 * MIB),
+        compiler_params=pltpu.CompilerParams(vmem_limit_bytes=VMEM_BACK * MIB),
         name="backward_attention",
-    )(y, kv, valid, q, *msgs)
+    )(y, q, *msgs, *kvs, *valids)
 
 
 def shift(count, by):
@@ -424,29 +434,32 @@
     meta = jnp.where(lane == 0, index // 64, jnp.where(lane == 1, index % 64, live_count[0]))
     own = jnp.concatenate([signal, meta.astype(bf16)], axis=1)
 
-    def absorbed(messages, base, state, last=False):
-        return absorb(messages, base, queries, w_in, w_kv, pos_table, state, last)
+    def absorbed(messages, state, last=False):
+        return absorb(messages, queries, w_in, w_kv, pos_table, state, last)
 
     cot = cotangent.reshape(pat_dev * lat_dev, width)
     cot_left = lax.ppermute(cot[lat_dev:], "tm", up1)
     cot_right = lax.ppermute(cot[: 3 * lat_dev], "tm", down1)
 
     below, above = own, own
-    at_hand, base, state = [own], 0, None
+    at_hand, state, kvs, valids = [own], None, [], []
     for step in range(1, NZ // 2 + 1):
         below = lax.ppermute(below, "z", shift(NZ, 1))
         if step < NZ // 2:
             above = lax.ppermute(above, "z", shift(NZ, -1))
-        state = list(absorbed(at_hand, base, state))
-        base += len(at_hand)
+        kv, valid, *state = absorbed(at_hand, state)
+        kvs.append(kv)
+        valids.append(valid)
         if step == 2:
-            below, above, state[1], cot_left, cot_right = lax.optimization_barrier(
-                (below, above, state[1], cot_left, cot_right)
+            below, above, valids[-1], cot_left, cot_right = lax.optimization_barrier(
+                (below, above, valids[-1], cot_left, cot_right)
             )
         elif step < NZ // 2:
-            below, above, state[1] = lax.optimization_barrier((below, above, state[1]))
+            below, above, valids[-1] = lax.optimization_barrier((below, above, valids[-1]))
         at_hand = [below, above] if step < NZ // 2 else [below]
-    kv, valid, *parts = absorbed(at_hand, base, state, last=True)
+    kv, valid, *parts = absorbed(at_hand, state, last=True)
+    kvs.append(kv)
+    valids.append(valid)
 
     received = [lax.ppermute(parts[s], "y", shift(NY, -s)) for s in range(1, NY)]
     att, stats = combine([parts[0]] + received)
@@ -462,7 +475,7 @@
 
     msg = msg.reshape(pat_dev, lat_dev, width + 128)
     msgs = [msg] + [lax.ppermute(msg, "y", shift(NY, s)) for s in range(1, NY)]
-    dq = backward_attention(y.reshape(1), kv, valid, queries, msgs)
+    dq = backward_attention(y.reshape(1), kvs, valids, queries, msgs)
 
     pieces = lax.all_to_all(dq, ("y", "tm"), 0, 0, tiled=True)
     dq_row = jnp.sum(pieces, axis=0, keepdims=True).astype(bf16)

time: 187 us -> 147 us (0.79)
  Pallas kernels: 73.1 us -> 51.9 us
  local copies, waits for them, and re-layouts: 24.3 us -> 5.12 us
    unnamed x24 -> x16, local copies, waits for them, and re-layouts: 23.4 us -> 4.22 us
    pallas_call x5, Pallas kernels: 54 us -> 35.1 us  [absorb(): pl.pallas_call(functools.partial(absorb_kernel, fresh=fresh, last=last, c...]
    pallas_call x1, Pallas kernels: 15.9 us -> 12.2 us  [backward_attention(): pl.pallas_call(functools.partial(backward_kernel, slots=len(msgs)), grid=...]
  transfers between devices with their start and end apart: 18 -> 18, of which waited for: 6 -> 6; matrix products, arithmetic and copies ran while one was open for 1% -> 1% of each run, Pallas kernels for 26% -> 20%
where the time goes in v3:
time: 147 us; the launch traced here: 146 us
  Pallas kernels  51.9 us (35%)
  blocking collectives  39.2 us (27%)
  starting transfers between devices  35.4 us (24%)
  waiting for transfers between devices  9.87 us (7%)
  local copies, waits for them, and re-layouts  5.12 us (3%)
  other arithmetic  1.83 us (1%)
  between operations  1.59 us (1%)
    pallas_call x5, Pallas kernels, absorb(): pl.pallas_call(functools.partial(absorb_kernel, fresh=fresh, last=last, c...  35.1 us
    all_to_all x1, blocking collectives, local(): dq_all = lax.all_to_all(copies, ('y', 'z', 'tm'), 0, 0, tiled=True)  23.9 us
    all_to_all x1, blocking collectives, local(): pieces = lax.all_to_all(dq, ('y', 'tm'), 0, 0, tiled=True)  15.3 us
    pallas_call x1, Pallas kernels, backward_attention(): pl.pallas_call(functools.partial(backward_kernel, slots=len(msgs)), grid=...  12.2 us
    ppermute x3, starting transfers between devices, local(): above = lax.ppermute(above, 'z', shift(NZ, -1))  9.35 us
    ppermute x3, starting transfers between devices, local(): lax.ppermute(parts[s], 'y', shift(NY, -s))  5.68 us
    ppermute x1, starting transfers between devices, local(): left = lax.ppermute(chip[2 * lat_dev:], 'tm', up2)  5.38 us
    ppermute x1, starting transfers between devices, local(): cot_left = lax.ppermute(cot[lat_dev:], 'tm', up1)  4.52 us
  transfers between devices with their start and end apart: 18, of which 6 were waited for; matrix products, arithmetic and copies ran while one was open for 1% of the time, Pallas kernels for 20%

profile of v3, /device:TPU:1, one launch (start us, length us, event | category | flops | bytes accessed | tf_op | source)
XLA Modules:
  0.0 146.2 jit_solution(3575642720176880235)
XLA Ops:
  0.6 0.0 copy-start
  0.7 0.7 and_select_fusion.1
  2.1 0.1 select_convert_fusion
  2.2 0.9 pad_maximum_fusion.refs_0_
  3.1 2.5 %collective-permute-start = (bf16[256,256]{1,0:T(8,128)(2,1)S(1)}, bf16[256,256]{1,0:T(8,128)(2,1)S(1)}, u32[]{:S(2)}, u32[]{:S(2)}) collective-permute-start(bf16[256,256]{1,0:T(8,128)(2,1)S(1)} %pad_maximum_fusion.refs_0_), channel_id=1, source_target_pairs={{0,8},{8,16},{16,24},{24,32},{32,40},{40,48},{48,56},{56,0},{1,9},... | collective-permute-start | bytes 393224 | tf_op jit(solution)/shard_map/ppermute | solution.py:447
  5.6 4.0 %collective-permute-start.1 = (bf16[256,256]{1,0:T(8,128)(2,1)S(1)}, bf16[256,256]{1,0:T(8,128)(2,1)S(1)}, u32[]{:S(2)}, u32[]{:S(2)}) collective-permute-start(bf16[256,256]{1,0:T(8,128)(2,1)S(1)} %pad_maximum_fusion.refs_0_), channel_id=1, source_target_pairs={{0,56},{8,0},{16,8},{24,16},{32,24},{40,32},{48,40},{56,48},{1,57}... | collective-permute-start | bytes 393224 | tf_op jit(solution)/shard_map/ppermute | solution.py:449
  9.6 0.7 dynamic-slice_bitcast_fusion.3
  10.4 0.0 copy-done
  10.4 0.2 convolution_convert_fusion.refs_1_.refs_2_.q_ref
  10.6 2.2 %copy-done.1 = bf16[4096,512]{1,0:T(8,128)(2,1)S(1)} copy-done((bf16[4096,512]{1,0:T(8,128)(2,1)S(1)}, bf16[4096,512]{1,0:T(8,128)(2,1)}, u32[]{:S(2)}) %copy-start.1) | copy-done | bytes 4194328
  12.8 1.2 copy-done.3
  14.0 0.8 copy-done.4
  14.7 4.1 %absorb.5 = (bf16[4,256,1024]{2,1,0:T(8,128)(2,1)}, f32[8,256]{1,0:T(8,128)S(1)}, f32[4,256,512]{2,1,0:T(8,128)S(1)}, f32[4,256,128]{2,1,0:T(8,128)S(1)}) custom-call(bf16[256,256]{1,0:T(8,128)(2,1)S(1)} %pad_maximum_fusion.refs_0_, bf16[32,512]{1,0:T(8,128)(2,1)S(1)} %convolution_convert_fusion.refs_1_.refs_2_.q_ref, bf16[32,512]{1,0:T(8,128)(2,1)S(1)} %copy-done.4, ...), custom_call_target="tpu_custom_call" | custom-call | tf_op jit(solution)/shard_map/absorb/pallas_call | solution.py:204
  18.8 0.0 collective-permute-done.refs_0_
  18.9 0.0 collective-permute-done.1.refs_1_
  18.9 0.1 collective-permute-start.2
  19.0 2.7 %collective-permute-start.3 = (bf16[256,256]{1,0:T(8,128)(2,1)S(1)}, bf16[256,256]{1,0:T(8,128)(2,1)S(1)}, u32[]{:S(2)}, u32[]{:S(2)}) collective-permute-start(bf16[256,256]{1,0:T(8,128)(2,1)S(1)} %collective-permute-done.1.refs_1_), channel_id=1, source_target_pairs={{0,56},{8,0},{16,8},{24,16},{32,24},{40,32},{48,40},{56,48},{1,57}... | collective-permute-start | bytes 393224 | tf_op jit(solution)/shard_map/ppermute | solution.py:449
  21.6 4.5 %collective-permute-start.4 = (bf16[24,512]{1,0:T(8,128)(2,1)S(1)}, bf16[24,512]{1,0:T(8,128)(2,1)S(1)}, u32[]{:S(2)}, u32[]{:S(2)}) collective-permute-start(bf16[24,512]{1,0:T(8,128)(2,1)S(1)} %get-tuple-element.83), channel_id=1, source_target_pairs={{0,1},{1,2},{2,3},{3,4},{4,5},{5,6},{6,7},{8,9},{9,10},{10,11},{11... | collective-permute-start | bytes 73736 | tf_op jit(solution)/shard_map/ppermute | solution.py:441
  26.2 1.9 %collective-permute-start.5 = (bf16[24,512]{1,0:T(8,128)(2,1)S(1)}, bf16[24,512]{1,0:T(8,128)(2,1)S(1)}, u32[]{:S(2)}, u32[]{:S(2)}) collective-permute-start(bf16[24,512]{1,0:T(8,128)(2,1)S(1)} %get-tuple-element.82), channel_id=1, source_target_pairs={{1,0},{2,1},{3,2},{4,3},{5,4},{6,5},{7,6},{9,8},{10,9},{11,10},{12... | collective-permute-start | bytes 73736 | tf_op jit(solution)/shard_map/ppermute | solution.py:442
  28.1 0.0 copy-done.2
  28.1 8.5 %absorb.6 = (bf16[4,512,1024]{2,1,0:T(8,128)(2,1)}, f32[8,512]{1,0:T(8,128)S(1)}, f32[4,256,512]{2,1,0:T(8,128)S(1)}, f32[4,256,128]{2,1,0:T(8,128)S(1)}) custom-call(bf16[256,256]{1,0:T(8,128)(2,1)S(1)} %collective-permute-done.refs_0_, bf16[256,256]{1,0:T(8,128)(2,1)S(1)} %collective-permute-done.1.refs_1_, ...), custom_call_target="tpu_custom_call", output_to_operand_aliasing={{2}: (6, {}), {3}: (7, {})} | custom-call | tf_op jit(solution)/shard_map/absorb/pallas_call | solution.py:204
  36.6 0.0 collective-permute-done.4.cl_ref
  36.6 0.0 collective-permute-done.5.cr_ref
  36.6 0.0 collective-permute-done.2.refs_0_
  36.6 0.0 collective-permute-done.3.refs_1_
  36.6 0.1 collective-permute-start.6
  36.7 2.7 %collective-permute-start.7 = (bf16[256,256]{1,0:T(8,128)(2,1)S(1)}, bf16[256,256]{1,0:T(8,128)(2,1)S(1)}, u32[]{:S(2)}, u32[]{:S(2)}) collective-permute-start(bf16[256,256]{1,0:T(8,128)(2,1)S(1)} %collective-permute-done.3.refs_1_), channel_id=1, source_target_pairs={{0,56},{8,0},{16,8},{24,16},{32,24},{40,32},{48,40},{56,48},{1,57}... | collective-permute-start | bytes 393224 | tf_op jit(solution)/shard_map/ppermute | solution.py:449
  39.4 8.5 %absorb.7 = (bf16[4,512,1024]{2,1,0:T(8,128)(2,1)}, f32[8,512]{1,0:T(8,128)S(1)}, f32[4,256,512]{2,1,0:T(8,128)S(1)}, f32[4,256,128]{2,1,0:T(8,128)S(1)}) custom-call(bf16[256,256]{1,0:T(8,128)(2,1)S(1)} %collective-permute-done.2.refs_0_, bf16[256,256]{1,0:T(8,128)(2,1)S(1)} %collective-permute-done.3.refs_1_, ...), custom_call_target="tpu_custom_call", output_to_operand_aliasing={{2}: (6, {}), {3}: (7, {})} | custom-call | tf_op jit(solution)/shard_map/absorb/pallas_call | solution.py:204
  47.8 0.0 collective-permute-done.6.refs_0_
  47.8 0.0 collective-permute-done.7.refs_1_
  47.8 0.1 collective-permute-start.8
  47.9 8.5 %absorb.8 = (bf16[4,512,1024]{2,1,0:T(8,128)(2,1)}, f32[8,512]{1,0:T(8,128)S(1)}, f32[4,256,512]{2,1,0:T(8,128)S(1)}, f32[4,256,128]{2,1,0:T(8,128)S(1)}) custom-call(bf16[256,256]{1,0:T(8,128)(2,1)S(1)} %collective-permute-done.6.refs_0_, bf16[256,256]{1,0:T(8,128)(2,1)S(1)} %collective-permute-done.7.refs_1_, ...), custom_call_target="tpu_custom_call", output_to_operand_aliasing={{2}: (6, {}), {3}: (7, {})} | custom-call | tf_op jit(solution)/shard_map/absorb/pallas_call | solution.py:204
  56.4 0.0 collective-permute-done.8.refs_0_
  56.4 0.0 copy-start.5
  56.4 0.0 copy-start.7
  56.4 5.6 %absorb.9 = (bf16[4,256,1024]{2,1,0:T(8,128)(2,1)}, f32[8,256]{1,0:T(8,128)S(1)}, f32[4,8,640]{2,1,0:T(8,128)S(1)}, f32[4,8,640]{2,1,0:T(8,128)S(1)}, f32[4,8,64...) custom-call(bf16[256,256]{1,0:T(8,128)(2,1)S(1)} %collective-permute-done.8.refs_0_, ...), custom_call_target="tpu_custom_call" | custom-call | tf_op jit(solution)/shard_map/absorb/pallas_call | solution.py:204
  62.0 3.0 %collective-permute-start.10 = (f32[4,8,640]{2,1,0:T(8,128)S(1)}, f32[4,8,640]{2,1,0:T(8,128)S(1)}, u32[]{:S(2)}, u32[]{:S(2)}) collective-permute-start(f32[4,8,640]{2,1,0:T(8,128)S(1)} %get-tuple-element.58), channel_id=1, source_target_pairs={{0,128},{64,192},{128,0},{192,64},{1,129},{65,193},{129,1},{193,65... | collective-permute-start | bytes 245768 | tf_op jit(solution)/shard_map/ppermute | solution.py:464
  65.0 0.4 collective-permute-start.11
  65.4 2.3 %collective-permute-start.9 = (f32[4,8,640]{2,1,0:T(8,128)S(1)}, f32[4,8,640]{2,1,0:T(8,128)S(1)}, u32[]{:S(2)}, u32[]{:S(2)}) collective-permute-start(f32[4,8,640]{2,1,0:T(8,128)S(1)} %get-tuple-element.57), channel_id=1, source_target_pairs={{0,192},{64,0},{128,64},{192,128},{1,193},{65,1},{129,65},{193,129... | collective-permute-start | bytes 245768 | tf_op jit(solution)/shard_map/ppermute | solution.py:464
  67.7 0.0 collective-permute-done.10.refs_2_
  67.7 1.8 %collective-permute-done.11.refs_3_ = f32[4,8,640]{2,1,0:T(8,128)S(1)} collective-permute-done((f32[4,8,640]{2,1,0:T(8,128)S(1)}, f32[4,8,640]{2,1,0:T(8,128)S(1)}, u32[]{:S(2)}, u32[]{:S(2)}) %collective-permute-start.11) | collective-permute-done | bytes 81952 | tf_op jit(solution)/shard_map/ppermute | solution.py:464
  69.5 0.0 collective-permute-done.9.refs_1_
  69.6 0.4 combine_parts.1
  70.0 0.1 collective-permute-start.12
  70.1 1.2 collective-permute-done.12.partner_ref
  71.3 5.4 %collective-permute-start.13 = (bf16[48,512]{1,0:T(8,128)(2,1)S(1)}, bf16[48,512]{1,0:T(8,128)(2,1)S(1)}, u32[]{:S(2)}, u32[]{:S(2)}) collective-permute-start(bf16[48,512]{1,0:T(8,128)(2,1)S(1)} %get-tuple-element.81), channel_id=1, source_target_pairs={{0,2},{1,3},{2,4},{3,5},{4,6},{5,7},{8,10},{9,11},{10,12},{11,13},... | collective-permute-start | bytes 147464 | tf_op jit(solution)/shard_map/ppermute | solution.py:469
  76.7 1.3 collective-permute-start.14
  78.0 0.0 collective-permute-done.13.left_ref
  78.0 3.5 %collective-permute-done.14.right_ref = bf16[48,512]{1,0:T(8,128)(2,1)S(1)} collective-permute-done((bf16[48,512]{1,0:T(8,128)(2,1)S(1)}, bf16[48,512]{1,0:T(8,128)(2,1)S(1)}, u32[]{:S(2)}, u32[]{:S(2)}) %collective-permute-start.14) | collective-permute-done | bytes 49184 | tf_op jit(solution)/shard_map/ppermute | solution.py:470
  81.5 0.0 copy-done.5
  81.5 4.2 %conv_stack.1 = (bf16[32,512]{1,0:T(8,128)(2,1)}, bf16[32,640]{1,0:T(8,128)(2,1)S(1)}) custom-call(s32[1]{0:T(128)} %bitcast.tm_ref, bf16[48,512]{1,0:T(8,128)(2,1)S(1)} %collective-permute-done.13.left_ref, bf16[32,512]{1,0:T(8,128)(2,1)S(1)} %get-tuple-element.60.own_ref, bf16[32,512]{1,0:T(8,128)(2,1)S(1)} %collective-permute-done.12.partner_ref, ...), custom_call_target="tpu_custom_call" | custom-call | tf_op jit(solution)/shard_map/conv_stack/pallas_call | solution.py:328
  85.8 0.3 collective-permute-start.15
  86.1 4.1 %collective-permute-start.16 = (bf16[4,8,640]{2,1,0:T(8,128)(2,1)S(1)}, bf16[4,8,640]{2,1,0:T(8,128)(2,1)S(1)}, u32[]{:S(2)}, u32[]{:S(2)}) collective-permute-start(bf16[4,8,640]{2,1,0:T(8,128)(2,1)S(1)} %bitcast.36), channel_id=1, source_target_pairs={{0,128},{64,192},{128,0},{192,64},{1,129},{65,193},{129,1},{193,65... | collective-permute-start | bytes 122888 | tf_op jit(solution)/shard_map/ppermute | solution.py:477
  90.2 0.0 collective-permute-start.17
  90.2 0.2 collective-permute-done.15.refs_1_
  90.4 1.6 %collective-permute-done.16.refs_2_ = bf16[4,8,640]{2,1,0:T(8,128)(2,1)S(1)} collective-permute-done((bf16[4,8,640]{2,1,0:T(8,128)(2,1)S(1)}, bf16[4,8,640]{2,1,0:T(8,128)(2,1)S(1)}, u32[]{:S(2)}, u32[]{:S(2)}) %collective-permute-start.16) | collective-permute-done | bytes 40992 | tf_op jit(solution)/shard_map/ppermute | solution.py:477
  92.0 1.5 %collective-permute-done.17.refs_3_ = bf16[4,8,640]{2,1,0:T(8,128)(2,1)S(1)} collective-permute-done((bf16[4,8,640]{2,1,0:T(8,128)(2,1)S(1)}, bf16[4,8,640]{2,1,0:T(8,128)(2,1)S(1)}, u32[]{:S(2)}, u32[]{:S(2)}) %collective-permute-start.17) | collective-permute-done | bytes 40992 | tf_op jit(solution)/shard_map/ppermute | solution.py:477
  93.5 12.2 %backward_attention.1 = f32[32,512]{1,0:T(8,128)S(1)} custom-call(s32[1]{0:T(128)} %bitcast.12.y_ref, bf16[32,512]{1,0:T(8,128)(2,1)S(1)} %convolution_convert_fusion.refs_1_.refs_2_.q_ref, bf16[4,8,640]{2,1,0:T(8,128)(2,1)S(1)} %bitcast.38, bf16[4,8,640]{2,1,0:T(8,128)(2,1)S(1)} %collective-permute-done.15.refs_1_, ...), custom_call_target="tpu_custom_call" | custom-call | tf_op jit(solution)/shard_map/backward_attention/pallas_call | solution.py:393
  105.7 0.1 copy.20
  105.8 15.3 %all_to_all.14 = f32[32,1,512]{2,1,0:T(1,128)S(1)} all-to-all(f32[32,1,512]{2,1,0:T(1,128)S(1)} %copy.20), channel_id=1, replica_groups=mesh['y'=4,'z'=8,'tm'=8] {'y','tm'}, dimensions={0} | all-to-all | bytes 131072 | tf_op jit(solution)/shard_map/all_to_all | solution.py:480
  121.0 0.1 reduce_sum.9
  121.1 0.1 broadcast_in_dim.30
  121.2 23.9 %all_to_all.15 = bf16[256,4,128]{2,1,0:T(4,128)(2,1)S(1)} all-to-all(bf16[256,4,128]{2,1,0:T(4,128)(2,1)S(1)} %broadcast_in_dim.30), channel_id=1, replica_groups=mesh['y'=4,'z'=8,'tm'=8] {'y','z','tm'}, dimensions={0} | all-to-all | bytes 524288 | tf_op jit(solution)/shard_map/all_to_all | solution.py:483
  145.1 1.1 fusion
  (11 shorter events, 0.0 us)
Async XLA Ops:
  0.6 9.7 %copy-start = (bf16[512,512]{1,0:T(8,128)(2,1)S(1)}, bf16[512,512]{1,0:T(8,128)(2,1)}, u32[]{:S(2)}) copy-start(bf16[512,512]{1,0:T(8,128)(2,1)} %param.19) | copy-start | bytes 1572868
  3.1 15.8 %collective-permute-start = (bf16[256,256]{1,0:T(8,128)(2,1)S(1)}, bf16[256,256]{1,0:T(8,128)(2,1)S(1)}, u32[]{:S(2)}, u32[]{:S(2)}) collective-permute-start(bf16[256,256]{1,0:T(8,128)(2,1)S(1)} %pad_maximum_fusion.refs_0_), channel_id=1, source_target_pairs={{0,8},{8,16},{16,24},{24,32},{32,40},{40,48},{48,56},{56,0},{1,9},... | collective-permute-start | bytes 393224 | tf_op jit(solution)/shard_map/ppermute | solution.py:447
  5.6 13.3 %collective-permute-start.1 = (bf16[256,256]{1,0:T(8,128)(2,1)S(1)}, bf16[256,256]{1,0:T(8,128)(2,1)S(1)}, u32[]{:S(2)}, u32[]{:S(2)}) collective-permute-start(bf16[256,256]{1,0:T(8,128)(2,1)S(1)} %pad_maximum_fusion.refs_0_), channel_id=1, source_target_pairs={{0,56},{8,0},{16,8},{24,16},{32,24},{40,32},{48,40},{56,48},{1,57}... | collective-permute-start | bytes 393224 | tf_op jit(solution)/shard_map/ppermute | solution.py:449
  10.6 2.2 %copy-start.1 = (bf16[4096,512]{1,0:T(8,128)(2,1)S(1)}, bf16[4096,512]{1,0:T(8,128)(2,1)}, u32[]{:S(2)}) copy-start(bf16[4096,512]{1,0:T(8,128)(2,1)} %refs_4_.9) | copy-start | bytes 12582916
  12.8 1.2 copy-start.3
  14.0 0.8 copy-start.4
  14.7 6.9 %copy-start.6 = (bf16[4,8,512]{2,1,0:T(8,128)(2,1)S(1)}, bf16[4,8,512]{2,1,0:T(8,128)(2,1)}, u32[]{:S(2)}) copy-start(bf16[4,8,512]{2,1,0:T(8,128)(2,1)} %param.23) | copy-start | bytes 98308
  14.7 13.3 %copy-start.2 = (bf16[4096,512]{1,0:T(8,128)(2,1)S(1)}, bf16[4096,512]{1,0:T(8,128)(2,1)}, u32[]{:S(2)}) copy-start(bf16[4096,512]{1,0:T(8,128)(2,1)} %refs_4_.9) | copy-start | bytes 12582916
  18.9 17.7 %collective-permute-start.2 = (bf16[256,256]{1,0:T(8,128)(2,1)S(1)}, bf16[256,256]{1,0:T(8,128)(2,1)S(1)}, u32[]{:S(2)}, u32[]{:S(2)}) collective-permute-start(bf16[256,256]{1,0:T(8,128)(2,1)S(1)} %collective-permute-done.refs_0_), channel_id=1, source_target_pairs={{0,8},{8,16},{16,24},{24,32},{32,40},{40,48},{48,56},{56,0},{1,9},... | collective-permute-start | bytes 393224 | tf_op jit(solution)/shard_map/ppermute | solution.py:447
  19.0 17.6 %collective-permute-start.3 = (bf16[256,256]{1,0:T(8,128)(2,1)S(1)}, bf16[256,256]{1,0:T(8,128)(2,1)S(1)}, u32[]{:S(2)}, u32[]{:S(2)}) collective-permute-start(bf16[256,256]{1,0:T(8,128)(2,1)S(1)} %collective-permute-done.1.refs_1_), channel_id=1, source_target_pairs={{0,56},{8,0},{16,8},{24,16},{32,24},{40,32},{48,40},{56,48},{1,57}... | collective-permute-start | bytes 393224 | tf_op jit(solution)/shard_map/ppermute | solution.py:449
  21.6 14.9 %collective-permute-start.4 = (bf16[24,512]{1,0:T(8,128)(2,1)S(1)}, bf16[24,512]{1,0:T(8,128)(2,1)S(1)}, u32[]{:S(2)}, u32[]{:S(2)}) collective-permute-start(bf16[24,512]{1,0:T(8,128)(2,1)S(1)} %get-tuple-element.83), channel_id=1, source_target_pairs={{0,1},{1,2},{2,3},{3,4},{4,5},{5,6},{6,7},{8,9},{9,10},{10,11},{11... | collective-permute-start | bytes 73736 | tf_op jit(solution)/shard_map/ppermute | solution.py:441
  26.2 10.4 %collective-permute-start.5 = (bf16[24,512]{1,0:T(8,128)(2,1)S(1)}, bf16[24,512]{1,0:T(8,128)(2,1)S(1)}, u32[]{:S(2)}, u32[]{:S(2)}) collective-permute-start(bf16[24,512]{1,0:T(8,128)(2,1)S(1)} %get-tuple-element.82), channel_id=1, source_target_pairs={{1,0},{2,1},{3,2},{4,3},{5,4},{6,5},{7,6},{9,8},{10,9},{11,10},{12... | collective-permute-start | bytes 73736 | tf_op jit(solution)/shard_map/ppermute | solution.py:442
  36.6 11.2 %collective-permute-start.6 = (bf16[256,256]{1,0:T(8,128)(2,1)S(1)}, bf16[256,256]{1,0:T(8,128)(2,1)S(1)}, u32[]{:S(2)}, u32[]{:S(2)}) collective-permute-start(bf16[256,256]{1,0:T(8,128)(2,1)S(1)} %collective-permute-done.2.refs_0_), channel_id=1, source_target_pairs={{0,8},{8,16},{16,24},{24,32},{32,40},{40,48},{48,56},{56,0},{1,9},... | collective-permute-start | bytes 393224 | tf_op jit(solution)/shard_map/ppermute | solution.py:447
  36.7 11.1 %collective-permute-start.7 = (bf16[256,256]{1,0:T(8,128)(2,1)S(1)}, bf16[256,256]{1,0:T(8,128)(2,1)S(1)}, u32[]{:S(2)}, u32[]{:S(2)}) collective-permute-start(bf16[256,256]{1,0:T(8,128)(2,1)S(1)} %collective-permute-done.3.refs_1_), channel_id=1, source_target_pairs={{0,56},{8,0},{16,8},{24,16},{32,24},{40,32},{48,40},{56,48},{1,57}... | collective-permute-start | bytes 393224 | tf_op jit(solution)/shard_map/ppermute | solution.py:449
  47.8 8.6 %collective-permute-start.8 = (bf16[256,256]{1,0:T(8,128)(2,1)S(1)}, bf16[256,256]{1,0:T(8,128)(2,1)S(1)}, u32[]{:S(2)}, u32[]{:S(2)}) collective-permute-start(bf16[256,256]{1,0:T(8,128)(2,1)S(1)} %collective-permute-done.6.refs_0_), channel_id=1, source_target_pairs={{0,8},{8,16},{16,24},{24,32},{32,40},{40,48},{48,56},{56,0},{1,9},... | collective-permute-start | bytes 393224 | tf_op jit(solution)/shard_map/ppermute | solution.py:447
  56.4 25.1 %copy-start.5 = (bf16[512,512]{1,0:T(8,128)(2,1)S(1)}, bf16[512,512]{1,0:T(8,128)(2,1)}, u32[]{:S(2)}) copy-start(bf16[512,512]{1,0:T(8,128)(2,1)} %w_out_ref.1) | copy-start | bytes 1572868
  56.4 25.1 %copy-start.7 = (f32[2,512]{1,0:T(2,128)S(1)}, f32[2,512]{1,0:T(2,128)}, u32[]{:S(2)}) copy-start(f32[2,512]{1,0:T(2,128)} %bias_ref.1) | copy-start | bytes 12292
  62.0 5.7 %collective-permute-start.10 = (f32[4,8,640]{2,1,0:T(8,128)S(1)}, f32[4,8,640]{2,1,0:T(8,128)S(1)}, u32[]{:S(2)}, u32[]{:S(2)}) collective-permute-start(f32[4,8,640]{2,1,0:T(8,128)S(1)} %get-tuple-element.58), channel_id=1, source_target_pairs={{0,128},{64,192},{128,0},{192,64},{1,129},{65,193},{129,1},{193,65... | collective-permute-start | bytes 245768 | tf_op jit(solution)/shard_map/ppermute | solution.py:464
  65.0 4.5 %collective-permute-start.11 = (f32[4,8,640]{2,1,0:T(8,128)S(1)}, f32[4,8,640]{2,1,0:T(8,128)S(1)}, u32[]{:S(2)}, u32[]{:S(2)}) collective-permute-start(f32[4,8,640]{2,1,0:T(8,128)S(1)} %get-tuple-element.59), channel_id=1, source_target_pairs={{0,64},{64,128},{128,192},{192,0},{1,65},{65,129},{129,193},{193,1... | collective-permute-start | bytes 245768 | tf_op jit(solution)/shard_map/ppermute | solution.py:464
  65.4 4.1 %collective-permute-start.9 = (f32[4,8,640]{2,1,0:T(8,128)S(1)}, f32[4,8,640]{2,1,0:T(8,128)S(1)}, u32[]{:S(2)}, u32[]{:S(2)}) collective-permute-start(f32[4,8,640]{2,1,0:T(8,128)S(1)} %get-tuple-element.57), channel_id=1, source_target_pairs={{0,192},{64,0},{128,64},{192,128},{1,193},{65,1},{129,65},{193,129... | collective-permute-start | bytes 245768 | tf_op jit(solution)/shard_map/ppermute | solution.py:464
  70.0 1.3 collective-permute-start.12
  71.3 6.7 %collective-permute-start.13 = (bf16[48,512]{1,0:T(8,128)(2,1)S(1)}, bf16[48,512]{1,0:T(8,128)(2,1)S(1)}, u32[]{:S(2)}, u32[]{:S(2)}) collective-permute-start(bf16[48,512]{1,0:T(8,128)(2,1)S(1)} %get-tuple-element.81), channel_id=1, source_target_pairs={{0,2},{1,3},{2,4},{3,5},{4,6},{5,7},{8,10},{9,11},{10,12},{11,13},... | collective-permute-start | bytes 147464 | tf_op jit(solution)/shard_map/ppermute | solution.py:469
  76.7 4.8 %collective-permute-start.14 = (bf16[48,512]{1,0:T(8,128)(2,1)S(1)}, bf16[48,512]{1,0:T(8,128)(2,1)S(1)}, u32[]{:S(2)}, u32[]{:S(2)}) collective-permute-start(bf16[48,512]{1,0:T(8,128)(2,1)S(1)} %get-tuple-element.80), channel_id=1, source_target_pairs={{2,0},{3,1},{4,2},{5,3},{6,4},{7,5},{10,8},{11,9},{12,10},{13,11},... | collective-permute-start | bytes 147464 | tf_op jit(solution)/shard_map/ppermute | solution.py:470
  85.8 4.6 %collective-permute-start.15 = (bf16[4,8,640]{2,1,0:T(8,128)(2,1)S(1)}, bf16[4,8,640]{2,1,0:T(8,128)(2,1)S(1)}, u32[]{:S(2)}, u32[]{:S(2)}) collective-permute-start(bf16[4,8,640]{2,1,0:T(8,128)(2,1)S(1)} %bitcast.35), channel_id=1, source_target_pairs={{0,64},{64,128},{128,192},{192,0},{1,65},{65,129},{129,193},{193,1... | collective-permute-start | bytes 122888 | tf_op jit(solution)/shard_map/ppermute | solution.py:477
  86.1 5.9 %collective-permute-start.16 = (bf16[4,8,640]{2,1,0:T(8,128)(2,1)S(1)}, bf16[4,8,640]{2,1,0:T(8,128)(2,1)S(1)}, u32[]{:S(2)}, u32[]{:S(2)}) collective-permute-start(bf16[4,8,640]{2,1,0:T(8,128)(2,1)S(1)} %bitcast.36), channel_id=1, source_target_pairs={{0,128},{64,192},{128,0},{192,64},{1,129},{65,193},{129,1},{193,65... | collective-permute-start | bytes 122888 | tf_op jit(solution)/shard_map/ppermute | solution.py:477
  90.2 3.3 %collective-permute-start.17 = (bf16[4,8,640]{2,1,0:T(8,128)(2,1)S(1)}, bf16[4,8,640]{2,1,0:T(8,128)(2,1)S(1)}, u32[]{:S(2)}, u32[]{:S(2)}) collective-permute-start(bf16[4,8,640]{2,1,0:T(8,128)(2,1)S(1)} %bitcast.37), channel_id=1, source_target_pairs={{0,192},{64,0},{128,64},{192,128},{1,193},{65,1},{129,65},{193,129... | collective-permute-start | bytes 122888 | tf_op jit(solution)/shard_map/ppermute | solution.py:477
